TPU v7x, 256 devices: a whole 4x4x8 slice. The times are simulated.
256 devices in a mesh: depth: 256 (over x, y, z, core).
Axes of the slice: x: 4, y: 4, z: 8, core: 2. Of those that a mesh axis runs over, the one named last changes fastest.
Arguments:
- w_in: bfloat16 [512, 512, 1024], P('depth'), may hold values from -0.25 to 0.25
- w_out: bfloat16 [512, 1024, 512], P('depth'), may hold values from -0.0234375 to 0.0234375
- checkpoint: bfloat16 [256, 256, 512], P('depth'), may hold values from -6 to 6
- guess: float32 [256, 256, 512], P('depth'), may hold values from -6 to 6
- terminal: float32 [256, 512], replicated, may hold values from -6 to 6
Outputs:
- adjoint: float32 [512, 256, 512], P('depth')
- grad_in: bfloat16 [512, 512, 1024], P('depth')
- grad_out: bfloat16 [512, 1024, 512], P('depth')
All inputs are finite; a program needn't handle non-finite values.
Results may differ from a plain program's by a relative error of at most 0.017.
Values sent between devices are 32-bit elements; how exact they have to be, the bound alone decides.
A program may use at most 64 MiB of HBM per device.

v0:
```python
import jax
import jax.numpy as jnp
from jax import lax
from jax.sharding import PartitionSpec as P

LEVELS = 4


def shifted(block, axis, distance):
    devices = range(lax.axis_size(axis))
    route = [(i - distance, i) for i in devices if i - distance in devices]
    return lax.ppermute(block, axis, route)


def tangent_of(vector, w_second, slope):
    product = jnp.dot(vector.astype(jnp.bfloat16), w_second.T, preferred_element_type=jnp.float32)
    return (product * slope).astype(jnp.bfloat16)


def apply_layer(vector, w_first, w_second, slope, factor):
    tangent = tangent_of(vector, w_second, slope)
    return (
        vector + factor * jnp.dot(tangent, w_first.T, preferred_element_type=jnp.float32),
        tangent,
    )


def local(w_in, w_out, checkpoint, guess, terminal):
    count = lax.axis_size("depth")
    place = lax.axis_index("depth")
    at_end = place == count - 1
    start = checkpoint[0]
    h_zero = jnp.tanh(jnp.dot(start, w_in[0], preferred_element_type=jnp.float32))
    act_zero = h_zero.astype(jnp.bfloat16)
    upper = start.astype(jnp.float32) + jnp.dot(
        act_zero, w_out[0], preferred_element_type=jnp.float32
    )
    upper_b = upper.astype(jnp.bfloat16)
    h_one = jnp.tanh(jnp.dot(upper_b, w_in[1], preferred_element_type=jnp.float32))
    act_one = h_one.astype(jnp.bfloat16)
    slope_zero = 1.0 - h_zero * h_zero
    slope_one = 1.0 - h_one * h_one

    def fine_next(values):
        moved = shifted(values, "depth", -1)
        return moved + jnp.where(at_end, terminal, jnp.zeros_like(terminal))

    def coarse_next(values, dist):
        return shifted(values, "depth", -dist)

    def cycle(level, rhs):
        dist = 2 ** (level - 1)
        active = place % dist == 0
        is_c = place % (2 * dist) == 0
        is_f = jnp.logical_and(active, jnp.logical_not(is_c))
        factor = float(2**level)

        def relax(values, mask):
            value, unused = apply_layer(
                coarse_next(values, dist), w_in[0], w_out[0], slope_zero, factor
            )
            return jnp.where(mask, value + rhs, values)

        values = jnp.where(is_f, rhs, jnp.zeros_like(rhs))
        values = relax(values, is_c)
        values = relax(values, is_f)
        if level == LEVELS - 1:
            return values
        value, unused = apply_layer(
            coarse_next(values, dist), w_in[0], w_out[0], slope_zero, factor
        )
        resid = jnp.where(is_c, value + rhs - values, jnp.zeros_like(rhs))
        values = values + cycle(level + 1, resid)
        return relax(values, is_f)

    even_value = guess[0]
    above = fine_next(even_value)
    odd_value, unused = apply_layer(above, w_in[1], w_out[1], slope_one, 1.0)
    value, unused = apply_layer(odd_value, w_in[0], w_out[0], slope_zero, 1.0)
    resid = value + 0.0 - even_value
    even_value = even_value + cycle(1, resid)
    above = fine_next(even_value)
    odd_value, tangent_one = apply_layer(above, w_in[1], w_out[1], slope_one, 1.0)
    odd_value = odd_value + 0.0
    tangent_zero = tangent_of(odd_value, w_out[0], slope_zero)
    grad_first = jnp.stack(
        [
            jnp.dot(start.T, tangent_zero, preferred_element_type=jnp.float32).astype(jnp.bfloat16),
            jnp.dot(upper_b.T, tangent_one, preferred_element_type=jnp.float32).astype(
                jnp.bfloat16
            ),
        ]
    )
    grad_second = jnp.stack(
        [
            jnp.dot(
                act_zero.T, odd_value.astype(jnp.bfloat16), preferred_element_type=jnp.float32
            ).astype(jnp.bfloat16),
            jnp.dot(
                act_one.T, above.astype(jnp.bfloat16), preferred_element_type=jnp.float32
            ).astype(jnp.bfloat16),
        ]
    )
    adjoint = jnp.stack([even_value, odd_value])
    return (adjoint, grad_first, grad_second)


def solution(mesh):
    placed = (
        P("depth", None, None),
        P("depth", None, None),
        P("depth", None, None),
        P("depth", None, None),
        P(),
    )
    return jax.shard_map(
        local,
        mesh=mesh,
        in_specs=placed,
        out_specs=(P("depth", None, None), P("depth", None, None), P("depth", None, None)),
        check_vma=False,
    )
```

profile of v0, /device:TPU:4, one launch (start us, length us, event | category | flops | bytes accessed | tf_op | source)
XLA Modules:
  0.0 268.6 jit_solution(8585524880135114906)
XLA Ops:
  0.6 9.6 %collective-permute-start = (f32[256,512]{1,0:T(8,128)}, f32[256,512]{1,0:T(8,128)}, u32[]{:S(2)}, u32[]{:S(2)}) collective-permute-start(f32[256,512]{1,0:T(8,128)} %bitcast.118), channel_id=1, source_target_pairs={{1,0},{2,1},{3,2},{4,3},{5,4},{6,5},{7,6},{8,7},{9,8},{10,9},{11,1... | collective-permute-start | bytes 1572872 | tf_op jit(solution)/shard_map/ppermute | solution.py:12
  10.3 0.0 copy-start.7
  10.3 0.0 copy-start
  10.3 1.9 convolution_tanh_fusion.1
  12.2 0.0 copy-done.7
  12.2 1.7 fusion.54
  13.9 0.0 copy-done
  13.9 1.4 convolution_tanh_fusion
  15.3 1.9 collective-permute-done
  17.3 3.5 %convolution_add_fusion.2 = f32[256,512]{1,0:T(8,128)} fusion(f32[256,1024]{1,0:T(8,128)} %convolution_tanh_fusion, bf16[2,1024,512]{2,1,0:T(8,128)(2,1)} %param.6, bf16[2,512,1024]{2,1,0:T(8,128)(2,1)S(1)} %copy-done, f32[256,512]{1,0:T(8,128)} %collective-permute-done, f32[256,512]{1,0:T(8,128)} %param.9, pred[]{:T(512)S(6)} %eq.23), kind=kOutput, calls=%fused_computation.52 | convolution fusion | flops 538705920 | bytes 5768192 | tf_op jit(solution)/shard_map/dot_general | solution.py:23
  20.8 3.4 %broadcast_select_fusion.2 = (f32[256,512]{1,0:T(8,128)}, f32[256,512]{1,0:T(8,128)}) fusion(pred[]{:T(512)S(6)} %not.9, f32[1,256,512]{2,1,0:T(8,128)} %param.8, f32[256,512]{1,0:T(8,128)} %convolution_add_fusion.2, bf16[2,512,1024]{2,1,0:T(8,128)(2,1)S(1)} %copy-done, f32[256,1024]{1,0:T(8,128)S(1)} %convolution_tanh_fusion.1, ...), kind=kOutput, calls=%fused_computation.151 | convolution fusion | flops 538443776 | bytes 5767169 | tf_op jit(solution)/shard_map/dot_general | solution.py:23
  24.2 8.0 %collective-permute-start.1 = (f32[256,512]{1,0:T(8,128)}, f32[256,512]{1,0:T(8,128)}, u32[]{:S(2)}, u32[]{:S(2)}) collective-permute-start(f32[256,512]{1,0:T(8,128)} %get-tuple-element.6), channel_id=1, source_target_pairs={{1,0},{2,1},{3,2},{4,3},{5,4},{6,5},{7,6},{8,7},{9,8},{10,9},{11,1... | collective-permute-start | bytes 1572872 | tf_op jit(solution)/shard_map/ppermute | solution.py:12
  32.2 7.0 %collective-permute-done.1 = f32[256,512]{1,0:T(8,128)} collective-permute-done((f32[256,512]{1,0:T(8,128)}, f32[256,512]{1,0:T(8,128)}, u32[]{:S(2)}, u32[]{:S(2)}) %collective-permute-start.1) | collective-permute-done | bytes 524320 | tf_op jit(solution)/shard_map/ppermute | solution.py:12
  39.2 3.2 %fusion.53 = f32[256,512]{1,0:T(8,128)} fusion(f32[256,512]{1,0:T(8,128)} %get-tuple-element.7, f32[256,512]{1,0:T(8,128)} %collective-permute-done.1, pred[]{:T(512)S(6)} %eq.22, pred[]{:T(512)S(6)} %not.9, f32[256,1024]{1,0:T(8,128)S(1)} %convolution_tanh_fusion.1, bf16[2,512,1024]{2,1,0:T(8,128)(2,1)S(1)} %copy-done, bf16[2,1024,512]{2,1,0:T(8,128)(2,1)} %param.6), kind=kOutput, calls=%fused_computation.89 | convolution fusion | flops 538705920 | bytes 5242882 | tf_op jit(solution)/shard_map/dot_general | solution.py:23
  42.4 8.0 %collective-permute-start.2 = (f32[256,512]{1,0:T(8,128)}, f32[256,512]{1,0:T(8,128)}, u32[]{:S(2)}, u32[]{:S(2)}) collective-permute-start(f32[256,512]{1,0:T(8,128)} %fusion.53), channel_id=1, source_target_pairs={{1,0},{2,1},{3,2},{4,3},{5,4},{6,5},{7,6},{8,7},{9,8},{10,9},{11,1... | collective-permute-start | bytes 1572872 | tf_op jit(solution)/shard_map/ppermute | solution.py:12
  50.5 7.0 %collective-permute-done.2 = f32[256,512]{1,0:T(8,128)} collective-permute-done((f32[256,512]{1,0:T(8,128)}, f32[256,512]{1,0:T(8,128)}, u32[]{:S(2)}, u32[]{:S(2)}) %collective-permute-start.2) | collective-permute-done | bytes 524320 | tf_op jit(solution)/shard_map/ppermute | solution.py:12
  57.5 3.4 %fusion.51 = f32[256,512]{1,0:T(8,128)} fusion(f32[256,512]{1,0:T(8,128)} %fusion.53, f32[256,512]{1,0:T(8,128)} %get-tuple-element.7, f32[256,512]{1,0:T(8,128)} %collective-permute-done.2, pred[]{:T(512)S(6)} %not.9, f32[256,1024]{1,0:T(8,128)S(1)} %convolution_tanh_fusion.1, bf16[2,512,1024]{2,1,0:T(8,128)(2,1)S(1)} %copy-done, ...), kind=kOutput, calls=%fused_computation.87 | convolution fusion | flops 538574848 | bytes 5767169 | tf_op jit(solution)/shard_map/dot_general | solution.py:23
  60.8 7.9 %collective-permute-start.3 = (f32[256,512]{1,0:T(8,128)}, f32[256,512]{1,0:T(8,128)}, u32[]{:S(2)}, u32[]{:S(2)}) collective-permute-start(f32[256,512]{1,0:T(8,128)} %fusion.51), channel_id=1, source_target_pairs={{1,0},{2,1},{3,2},{4,3},{5,4},{6,5},{7,6},{8,7},{9,8},{10,9},{11,1... | collective-permute-start | bytes 1572872 | tf_op jit(solution)/shard_map/ppermute | solution.py:12
  68.7 7.0 %collective-permute-done.3 = f32[256,512]{1,0:T(8,128)} collective-permute-done((f32[256,512]{1,0:T(8,128)}, f32[256,512]{1,0:T(8,128)}, u32[]{:S(2)}, u32[]{:S(2)}) %collective-permute-start.3) | collective-permute-done | bytes 524320 | tf_op jit(solution)/shard_map/ppermute | solution.py:12
  75.7 3.6 %broadcast_select_fusion.1 = (f32[256,512]{1,0:T(8,128)}, f32[256,512]{1,0:T(8,128)}) fusion(pred[]{:T(512)S(6)} %and.27, f32[256,512]{1,0:T(8,128)} %fusion.51, f32[256,512]{1,0:T(8,128)} %get-tuple-element.7, f32[256,512]{1,0:T(8,128)} %collective-permute-done.3, bf16[2,512,1024]{2,1,0:T(8,128)(2,1)S(1)} %copy-done, ...), kind=kOutput, calls=%fused_computation.150 | convolution fusion | flops 538836992 | bytes 6291458 | tf_op jit(solution)/shard_map/dot_general | solution.py:23
  79.3 1.9 collective-permute-start.4
  81.2 9.5 %collective-permute-done.4 = f32[256,512]{1,0:T(8,128)} collective-permute-done((f32[256,512]{1,0:T(8,128)}, f32[256,512]{1,0:T(8,128)}, u32[]{:S(2)}, u32[]{:S(2)}) %collective-permute-start.4) | collective-permute-done | bytes 524320 | tf_op jit(solution)/shard_map/ppermute | solution.py:12
  90.7 3.2 %fusion.46 = f32[256,512]{1,0:T(8,128)} fusion(f32[256,512]{1,0:T(8,128)} %get-tuple-element.9, f32[256,512]{1,0:T(8,128)} %collective-permute-done.4, pred[]{:T(512)S(6)} %eq.24, pred[]{:T(512)S(6)} %and.27, f32[256,1024]{1,0:T(8,128)S(1)} %convolution_tanh_fusion.1, bf16[2,512,1024]{2,1,0:T(8,128)(2,1)S(1)} %copy-done, bf16[2,1024,512]{2,1,0:T(8,128)(2,1)} %param.6), kind=kOutput, calls=%fused_computation.82 | convolution fusion | flops 538705920 | bytes 5242882 | tf_op jit(solution)/shard_map/dot_general | solution.py:23
  93.9 6.1 %collective-permute-start.5 = (f32[256,512]{1,0:T(8,128)}, f32[256,512]{1,0:T(8,128)}, u32[]{:S(2)}, u32[]{:S(2)}) collective-permute-start(f32[256,512]{1,0:T(8,128)} %fusion.46), channel_id=1, source_target_pairs={{2,0},{3,1},{4,2},{5,3},{6,4},{7,5},{8,6},{9,7},{10,8},{11,9},{12,... | collective-permute-start | bytes 1572872 | tf_op jit(solution)/shard_map/ppermute | solution.py:12
  100.0 8.5 %collective-permute-done.5 = f32[256,512]{1,0:T(8,128)} collective-permute-done((f32[256,512]{1,0:T(8,128)}, f32[256,512]{1,0:T(8,128)}, u32[]{:S(2)}, u32[]{:S(2)}) %collective-permute-start.5) | collective-permute-done | bytes 524320 | tf_op jit(solution)/shard_map/ppermute | solution.py:12
  108.5 3.4 %fusion.44 = f32[256,512]{1,0:T(8,128)} fusion(f32[256,512]{1,0:T(8,128)} %fusion.46, f32[256,512]{1,0:T(8,128)} %get-tuple-element.9, f32[256,512]{1,0:T(8,128)} %collective-permute-done.5, pred[]{:T(512)S(6)} %and.27, f32[256,1024]{1,0:T(8,128)S(1)} %convolution_tanh_fusion.1, bf16[2,512,1024]{2,1,0:T(8,128)(2,1)S(1)} %copy-done, ...), kind=kOutput, calls=%fused_computation.80 | convolution fusion | flops 538574848 | bytes 5767169 | tf_op jit(solution)/shard_map/dot_general | solution.py:23
  111.9 8.0 %collective-permute-start.6 = (f32[256,512]{1,0:T(8,128)}, f32[256,512]{1,0:T(8,128)}, u32[]{:S(2)}, u32[]{:S(2)}) collective-permute-start(f32[256,512]{1,0:T(8,128)} %fusion.44), channel_id=1, source_target_pairs={{2,0},{3,1},{4,2},{5,3},{6,4},{7,5},{8,6},{9,7},{10,8},{11,9},{12,... | collective-permute-start | bytes 1572872 | tf_op jit(solution)/shard_map/ppermute | solution.py:12
  120.0 9.0 %collective-permute-done.6 = f32[256,512]{1,0:T(8,128)} collective-permute-done((f32[256,512]{1,0:T(8,128)}, f32[256,512]{1,0:T(8,128)}, u32[]{:S(2)}, u32[]{:S(2)}) %collective-permute-start.6) | collective-permute-done | bytes 524320 | tf_op jit(solution)/shard_map/ppermute | solution.py:12
  129.0 3.6 %broadcast_select_fusion = (f32[256,512]{1,0:T(8,128)}, f32[256,512]{1,0:T(8,128)}) fusion(pred[]{:T(512)S(6)} %and.29, f32[256,512]{1,0:T(8,128)} %fusion.44, f32[256,512]{1,0:T(8,128)} %get-tuple-element.9, f32[256,512]{1,0:T(8,128)} %collective-permute-done.6, bf16[2,512,1024]{2,1,0:T(8,128)(2,1)S(1)} %copy-done, ...), kind=kOutput, calls=%fused_computation.149 | convolution fusion | flops 538836992 | bytes 6291458 | tf_op jit(solution)/shard_map/dot_general | solution.py:23
  132.5 3.5 %collective-permute-start.7 = (f32[256,512]{1,0:T(8,128)}, f32[256,512]{1,0:T(8,128)}, u32[]{:S(2)}, u32[]{:S(2)}) collective-permute-start(f32[256,512]{1,0:T(8,128)} %get-tuple-element.10), channel_id=1, source_target_pairs={{4,0},{5,1},{6,2},{7,3},{8,4},{9,5},{10,6},{11,7},{12,8},{13,9},{1... | collective-permute-start | bytes 1572872 | tf_op jit(solution)/shard_map/ppermute | solution.py:12
  136.1 23.4 %collective-permute-done.7 = f32[256,512]{1,0:T(8,128)} collective-permute-done((f32[256,512]{1,0:T(8,128)}, f32[256,512]{1,0:T(8,128)}, u32[]{:S(2)}, u32[]{:S(2)}) %collective-permute-start.7) | collective-permute-done | bytes 524320 | tf_op jit(solution)/shard_map/ppermute | solution.py:12
  159.5 3.2 %fusion.39 = f32[256,512]{1,0:T(8,128)} fusion(f32[256,512]{1,0:T(8,128)} %get-tuple-element.11, f32[256,512]{1,0:T(8,128)} %collective-permute-done.7, pred[]{:T(512)S(6)} %eq.25, pred[]{:T(512)S(6)} %and.29, f32[256,1024]{1,0:T(8,128)S(1)} %convolution_tanh_fusion.1, bf16[2,512,1024]{2,1,0:T(8,128)(2,1)S(1)} %copy-done, bf16[2,1024,512]{2,1,0:T(8,128)(2,1)} %param.6), kind=kOutput, calls=%fused_computation.75 | convolution fusion | flops 538705920 | bytes 5242882 | tf_op jit(solution)/shard_map/dot_general | solution.py:23
  162.8 1.9 collective-permute-start.8
  164.7 15.2 %collective-permute-done.8 = f32[256,512]{1,0:T(8,128)} collective-permute-done((f32[256,512]{1,0:T(8,128)}, f32[256,512]{1,0:T(8,128)}, u32[]{:S(2)}, u32[]{:S(2)}) %collective-permute-start.8) | collective-permute-done | bytes 524320 | tf_op jit(solution)/shard_map/ppermute | solution.py:12
  179.9 3.6 %fusion.37 = f32[256,512]{1,0:T(8,128)} fusion(f32[256,512]{1,0:T(8,128)} %fusion.44, f32[256,512]{1,0:T(8,128)} %fusion.39, f32[256,512]{1,0:T(8,128)} %get-tuple-element.11, f32[256,512]{1,0:T(8,128)} %collective-permute-done.8, pred[]{:T(512)S(6)} %and.29, f32[256,1024]{1,0:T(8,128)S(1)} %convolution_tanh_fusion.1, ...), kind=kOutput, calls=%fused_computation.73 | convolution fusion | flops 538705920 | bytes 6291457 | tf_op jit(solution)/shard_map/dot_general | solution.py:23
  183.5 18.8 %collective-permute-start.9 = (f32[256,512]{1,0:T(8,128)}, f32[256,512]{1,0:T(8,128)}, u32[]{:S(2)}, u32[]{:S(2)}) collective-permute-start(f32[256,512]{1,0:T(8,128)} %fusion.37), channel_id=1, source_target_pairs={{2,0},{3,1},{4,2},{5,3},{6,4},{7,5},{8,6},{9,7},{10,8},{11,9},{12,... | collective-permute-start | bytes 1572872 | tf_op jit(solution)/shard_map/ppermute | solution.py:12
  202.2 11.4 %collective-permute-done.9 = f32[256,512]{1,0:T(8,128)} collective-permute-done((f32[256,512]{1,0:T(8,128)}, f32[256,512]{1,0:T(8,128)}, u32[]{:S(2)}, u32[]{:S(2)}) %collective-permute-start.9) | collective-permute-done | bytes 524320 | tf_op jit(solution)/shard_map/ppermute | solution.py:12
  213.7 3.6 %fusion.34 = f32[256,512]{1,0:T(8,128)} fusion(f32[256,512]{1,0:T(8,128)} %fusion.51, f32[256,512]{1,0:T(8,128)} %fusion.37, f32[256,512]{1,0:T(8,128)} %get-tuple-element.9, f32[256,512]{1,0:T(8,128)} %collective-permute-done.9, pred[]{:T(512)S(6)} %and.27, f32[256,1024]{1,0:T(8,128)S(1)} %convolution_tanh_fusion.1, bf16[2,512,1024]{2,1,0:T(8,128)(2,1)S(1)} %copy-done, ...), kind=kOutput, calls=%fused_computation.70 | convolution fusion | flops 538705920 | bytes 6291457 | tf_op jit(solution)/shard_map/dot_general | solution.py:23
  217.2 7.1 %collective-permute-start.10 = (f32[256,512]{1,0:T(8,128)}, f32[256,512]{1,0:T(8,128)}, u32[]{:S(2)}, u32[]{:S(2)}) collective-permute-start(f32[256,512]{1,0:T(8,128)} %fusion.34), channel_id=1, source_target_pairs={{1,0},{2,1},{3,2},{4,3},{5,4},{6,5},{7,6},{8,7},{9,8},{10,9},{11,1... | collective-permute-start | bytes 1572872 | tf_op jit(solution)/shard_map/ppermute | solution.py:12
  224.4 7.0 %collective-permute-done.10 = f32[256,512]{1,0:T(8,128)} collective-permute-done((f32[256,512]{1,0:T(8,128)}, f32[256,512]{1,0:T(8,128)}, u32[]{:S(2)}, u32[]{:S(2)}) %collective-permute-start.10) | collective-permute-done | bytes 524320 | tf_op jit(solution)/shard_map/ppermute | solution.py:12
  231.4 3.6 %fusion.31 = f32[256,512]{1,0:T(8,128)} fusion(f32[256,512]{1,0:T(8,128)} %fusion.34, f32[256,512]{1,0:T(8,128)} %get-tuple-element.7, f32[256,512]{1,0:T(8,128)} %collective-permute-done.10, pred[]{:T(512)S(6)} %not.9, f32[1,256,512]{2,1,0:T(8,128)} %param.8, f32[256,1024]{1,0:T(8,128)S(1)} %convolution_tanh_fusion.1, ...), kind=kOutput, calls=%fused_computation.67 | convolution fusion | flops 538705920 | bytes 6291457 | tf_op jit(solution)/shard_map/dot_general | solution.py:23
  234.9 8.2 %collective-permute-start.11 = (f32[256,512]{1,0:T(8,128)}, f32[256,512]{1,0:T(8,128)S(1)}, u32[]{:S(2)}, u32[]{:S(2)}) collective-permute-start(f32[256,512]{1,0:T(8,128)} %fusion.31), channel_id=1, source_target_pairs={{1,0},{2,1},{3,2},{4,3},{5,4},{6,5},{7,6},{8,7},{9,8},{10,9},{11,1... | collective-permute-start | bytes 1572872 | tf_op jit(solution)/shard_map/ppermute | solution.py:12
  243.1 6.8 %collective-permute-done.11 = f32[256,512]{1,0:T(8,128)S(1)} collective-permute-done((f32[256,512]{1,0:T(8,128)}, f32[256,512]{1,0:T(8,128)S(1)}, u32[]{:S(2)}, u32[]{:S(2)}) %collective-permute-start.11) | collective-permute-done | bytes 524320 | tf_op jit(solution)/shard_map/ppermute | solution.py:12
  249.9 0.1 fusion.138
  250.0 2.0 fusion.16
  252.0 0.0 copy-done.2
  252.0 0.0 copy-start.9
  252.1 1.5 fusion.3
  253.5 1.5 fusion.1
  255.0 0.0 copy-done.9
  255.0 0.5 convolution_add_fusion
  255.5 0.0 copy-start.3
  255.5 0.8 copy-done.3
  256.3 1.4 fusion.2
  257.7 0.5 copy-done.1
  258.2 0.0 copy-done.8
  258.2 2.8 %fusion = bf16[1,512,1024]{1,2,0:T(8,128)(2,1)} fusion(bf16[1,256,512]{2,1,0:T(8,128)(2,1)S(1)} %copy-done.8, f32[256,512]{1,0:T(8,128)} %copy-done.3, f32[256,1024]{1,0:T(8,128)S(1)} %convolution_tanh_fusion.1, bf16[2,1024,512]{2,1,0:T(8,128)(2,1)S(1)} %copy-done.1), kind=kOutput, calls=%fused_computation.6 | convolution fusion | flops 538574848 | bytes 3932160 | tf_op jit(solution)/shard_map/dot_general | solution.py:88
  261.0 1.7 pad_maximum_fusion
  262.8 2.4 copy.9
  265.2 0.0 copy-done.10
  265.2 1.0 pad_maximum_fusion.2
  266.2 0.6 copy-done.5
  266.8 0.3 copy-done.6
  267.1 1.5 pad_maximum_fusion.1
  (8 shorter events, 0.0 us)
Async XLA Ops:
  0.6 16.6 %collective-permute-start = (f32[256,512]{1,0:T(8,128)}, f32[256,512]{1,0:T(8,128)}, u32[]{:S(2)}, u32[]{:S(2)}) collective-permute-start(f32[256,512]{1,0:T(8,128)} %bitcast.118), channel_id=1, source_target_pairs={{1,0},{2,1},{3,2},{4,3},{5,4},{6,5},{7,6},{8,7},{9,8},{10,9},{11,1... | collective-permute-start | bytes 1572872 | tf_op jit(solution)/shard_map/ppermute | solution.py:12
  10.3 1.9 copy-start.7
  10.3 3.6 %copy-start = (bf16[2,512,1024]{2,1,0:T(8,128)(2,1)S(1)}, bf16[2,512,1024]{2,1,0:T(8,128)(2,1)}, u32[]{:S(2)}) copy-start(bf16[2,512,1024]{2,1,0:T(8,128)(2,1)} %param.5) | copy-start | bytes 6291460
  24.2 15.0 %collective-permute-start.1 = (f32[256,512]{1,0:T(8,128)}, f32[256,512]{1,0:T(8,128)}, u32[]{:S(2)}, u32[]{:S(2)}) collective-permute-start(f32[256,512]{1,0:T(8,128)} %get-tuple-element.6), channel_id=1, source_target_pairs={{1,0},{2,1},{3,2},{4,3},{5,4},{6,5},{7,6},{8,7},{9,8},{10,9},{11,1... | collective-permute-start | bytes 1572872 | tf_op jit(solution)/shard_map/ppermute | solution.py:12
  42.4 15.0 %collective-permute-start.2 = (f32[256,512]{1,0:T(8,128)}, f32[256,512]{1,0:T(8,128)}, u32[]{:S(2)}, u32[]{:S(2)}) collective-permute-start(f32[256,512]{1,0:T(8,128)} %fusion.53), channel_id=1, source_target_pairs={{1,0},{2,1},{3,2},{4,3},{5,4},{6,5},{7,6},{8,7},{9,8},{10,9},{11,1... | collective-permute-start | bytes 1572872 | tf_op jit(solution)/shard_map/ppermute | solution.py:12
  60.8 14.9 %collective-permute-start.3 = (f32[256,512]{1,0:T(8,128)}, f32[256,512]{1,0:T(8,128)}, u32[]{:S(2)}, u32[]{:S(2)}) collective-permute-start(f32[256,512]{1,0:T(8,128)} %fusion.51), channel_id=1, source_target_pairs={{1,0},{2,1},{3,2},{4,3},{5,4},{6,5},{7,6},{8,7},{9,8},{10,9},{11,1... | collective-permute-start | bytes 1572872 | tf_op jit(solution)/shard_map/ppermute | solution.py:12
  79.3 11.4 %collective-permute-start.4 = (f32[256,512]{1,0:T(8,128)}, f32[256,512]{1,0:T(8,128)}, u32[]{:S(2)}, u32[]{:S(2)}) collective-permute-start(f32[256,512]{1,0:T(8,128)} %get-tuple-element.8), channel_id=1, source_target_pairs={{2,0},{3,1},{4,2},{5,3},{6,4},{7,5},{8,6},{9,7},{10,8},{11,9},{12,... | collective-permute-start | bytes 1572872 | tf_op jit(solution)/shard_map/ppermute | solution.py:12
  93.9 14.6 %collective-permute-start.5 = (f32[256,512]{1,0:T(8,128)}, f32[256,512]{1,0:T(8,128)}, u32[]{:S(2)}, u32[]{:S(2)}) collective-permute-start(f32[256,512]{1,0:T(8,128)} %fusion.46), channel_id=1, source_target_pairs={{2,0},{3,1},{4,2},{5,3},{6,4},{7,5},{8,6},{9,7},{10,8},{11,9},{12,... | collective-permute-start | bytes 1572872 | tf_op jit(solution)/shard_map/ppermute | solution.py:12
  111.9 17.1 %collective-permute-start.6 = (f32[256,512]{1,0:T(8,128)}, f32[256,512]{1,0:T(8,128)}, u32[]{:S(2)}, u32[]{:S(2)}) collective-permute-start(f32[256,512]{1,0:T(8,128)} %fusion.44), channel_id=1, source_target_pairs={{2,0},{3,1},{4,2},{5,3},{6,4},{7,5},{8,6},{9,7},{10,8},{11,9},{12,... | collective-permute-start | bytes 1572872 | tf_op jit(solution)/shard_map/ppermute | solution.py:12
  132.5 27.0 %collective-permute-start.7 = (f32[256,512]{1,0:T(8,128)}, f32[256,512]{1,0:T(8,128)}, u32[]{:S(2)}, u32[]{:S(2)}) collective-permute-start(f32[256,512]{1,0:T(8,128)} %get-tuple-element.10), channel_id=1, source_target_pairs={{4,0},{5,1},{6,2},{7,3},{8,4},{9,5},{10,6},{11,7},{12,8},{13,9},{1... | collective-permute-start | bytes 1572872 | tf_op jit(solution)/shard_map/ppermute | solution.py:12
  162.8 17.1 %collective-permute-start.8 = (f32[256,512]{1,0:T(8,128)}, f32[256,512]{1,0:T(8,128)}, u32[]{:S(2)}, u32[]{:S(2)}) collective-permute-start(f32[256,512]{1,0:T(8,128)} %fusion.39), channel_id=1, source_target_pairs={{4,0},{5,1},{6,2},{7,3},{8,4},{9,5},{10,6},{11,7},{12,8},{13,9},{1... | collective-permute-start | bytes 1572872 | tf_op jit(solution)/shard_map/ppermute | solution.py:12
  183.5 30.2 %collective-permute-start.9 = (f32[256,512]{1,0:T(8,128)}, f32[256,512]{1,0:T(8,128)}, u32[]{:S(2)}, u32[]{:S(2)}) collective-permute-start(f32[256,512]{1,0:T(8,128)} %fusion.37), channel_id=1, source_target_pairs={{2,0},{3,1},{4,2},{5,3},{6,4},{7,5},{8,6},{9,7},{10,8},{11,9},{12,... | collective-permute-start | bytes 1572872 | tf_op jit(solution)/shard_map/ppermute | solution.py:12
  217.2 14.1 %collective-permute-start.10 = (f32[256,512]{1,0:T(8,128)}, f32[256,512]{1,0:T(8,128)}, u32[]{:S(2)}, u32[]{:S(2)}) collective-permute-start(f32[256,512]{1,0:T(8,128)} %fusion.34), channel_id=1, source_target_pairs={{1,0},{2,1},{3,2},{4,3},{5,4},{6,5},{7,6},{8,7},{9,8},{10,9},{11,1... | collective-permute-start | bytes 1572872 | tf_op jit(solution)/shard_map/ppermute | solution.py:12
  234.9 17.1 %copy-start.2 = (f32[256,1024]{1,0:T(8,128)S(1)}, f32[256,1024]{1,0:T(8,128)}, u32[]{:S(2)}) copy-start(f32[256,1024]{1,0:T(8,128)} %convolution_tanh_fusion) | copy-start | bytes 3145732
  234.9 15.0 %collective-permute-start.11 = (f32[256,512]{1,0:T(8,128)}, f32[256,512]{1,0:T(8,128)S(1)}, u32[]{:S(2)}, u32[]{:S(2)}) collective-permute-start(f32[256,512]{1,0:T(8,128)} %fusion.31), channel_id=1, source_target_pairs={{1,0},{2,1},{3,2},{4,3},{5,4},{6,5},{7,6},{8,7},{9,8},{10,9},{11,1... | collective-permute-start | bytes 1572872 | tf_op jit(solution)/shard_map/ppermute | solution.py:12
  252.0 2.9 %copy-start.9 = (f32[256,512]{1,0:T(8,128)S(1)}, f32[256,512]{1,0:T(8,128)}, u32[]{:S(2)}) copy-start(f32[256,512]{1,0:T(8,128)} %param.9) | copy-start | bytes 1572868
  255.5 0.8 copy-start.3
  256.3 1.9 copy-start.1
  256.3 2.0 copy-start.8
  262.8 2.4 copy-start.4
  262.8 2.4 copy-start.10
  265.2 1.6 copy-start.5
  265.2 1.9 copy-start.6
where the time goes:
time: 269 us
  waiting for transfers between devices  114 us (42%)
  starting transfers between devices  89.2 us (33%)
  matrix products  55.8 us (21%)
  local copies, waits for them, and re-layouts  4.58 us (2%)
  other arithmetic  4.38 us (2%)
    ppermute x12, waiting for transfers between devices, shifted(): return lax.ppermute(block, axis, route)  114 us
    ppermute x12, starting transfers between devices, shifted(): return lax.ppermute(block, axis, route)  89.2 us
    dot_general x13, matrix products, apply_layer(): jnp.dot(tangent, w_first.T, preferred_element_type=jnp.float32)  41.7 us
  transfers between devices with their start and end apart: 12, of which 12 were waited for; matrix products, arithmetic and copies ran while one was open for 2% of the time, Pallas kernels for 0%

commit v1 on v0

v1 whole, which is shorter than its diff:
```python
import functools

import jax
import jax.numpy as jnp
from jax import lax
from jax.experimental import pallas as pl
from jax.experimental.pallas import tpu as pltpu
from jax.sharding import PartitionSpec as P

MESH = pl.DeviceIdType.MESH
BF = jnp.bfloat16
F32 = jnp.float32

GUESS_IN, GUESS, R1, VC, Y, R2, WC, U, R3, X, XUP, W_IN, W, E = range(14)
MESSAGES = 14


def matmul(a, b):
    return jnp.dot(a, b, preferred_element_type=F32)


def kernel(
    count, rows_per, wi_h, wo_h, cp_h, gs_h, tm_h, adj_h, gi_h, go_h,
    wi, wo, wit, wot, cp, gs, state_one, act, slope, tang,
    g_next, r1, r1_next, vc, vc_next, y, r2, r2_next, wc, wc_next, u, r3, r3_next, x, x_next, x_up, w, w_next, w_above,
    e_next, adj, gi, go, load_sem, store_sem, send_sem, recv_sem,
):
    n = lax.axis_index("depth")
    core = lax.rem(n, 2)
    even = core == 0
    chip_odd = lax.rem(n, 4) == 2
    chip_even = lax.rem(n, 4) == 0
    pair_odd = lax.rem(n, 8) == 4
    pair_even = lax.rem(n, 8) == 0
    total = cp.shape[0]
    chunks = total // rows_per

    def rows_of(k):
        return pl.ds(pl.multiple_of(k * rows_per, rows_per), rows_per)

    def message(kind, k, source, target, peer, receives=None):
        rows = rows_of(k)
        return pltpu.make_async_remote_copy(
            src_ref=source.at[rows],
            dst_ref=target.at[rows],
            send_sem=send_sem.at[kind, k],
            recv_sem=recv_sem.at[kind if receives is None else receives, k],
            device_id=(peer,),
            device_id_type=MESH,
        )

    def arrived(kind, k, target):
        message(kind, k, target, target, n).wait_recv()

    def each(body):
        def step(k, carry):
            body(k, rows_of(k))
            return carry

        lax.fori_loop(0, chunks, step, 0)

    def tangent(value, layer, rows):
        return (matmul(value.astype(BF), wot[layer]) * slope[layer, rows, :]).astype(BF)

    def moved(value, layer, rows):
        return matmul(tangent(value, layer, rows), wit[layer])

    loads = [
        pltpu.make_async_copy(source, target, load_sem.at[place])
        for place, (source, target) in enumerate(
            (
                (cp_h.at[0], cp),
                (wi_h.at[0], wi.at[0]),
                (wo_h.at[0], wo.at[0]),
                (wi_h.at[1], wi.at[1]),
                (wo_h.at[1], wo.at[1]),
                (gs_h.at[0], gs),
            )
        )
    ]
    for copy in loads:
        copy.start()

    barrier = pltpu.get_barrier_semaphore()
    peers = (
        (n + 1, jnp.logical_and(n >= 0, n + 1 < count)),
        (n - 1, n >= 1),
        (n + 2, jnp.logical_and(even, n + 2 < count)),
        (n - 2, jnp.logical_and(even, n >= 2)),
        (n + 4, jnp.logical_and(chip_even, n + 4 < count)),
        (n - 4, jnp.logical_and(chip_even, n >= 4)),
    )
    for peer, there in peers:

        @pl.when(there)
        def _(peer=peer):
            pl.semaphore_signal(barrier, inc=1, device_id=(peer,), device_id_type=MESH)

    greeted = sum(jnp.where(there, 1, 0) for _, there in peers)
    pl.semaphore_wait(barrier, greeted)

    @pl.when(jnp.logical_not(even))
    def _():
        each(lambda k, rows: message(GUESS_IN, k, gs_h.at[0], g_next, n - 1).start())

    @pl.when(jnp.logical_and(even, n >= 1))
    def _():
        each(lambda k, rows: message(GUESS, k, gs_h.at[0], g_next, n - 1).start())

    def terminal_copy(k):
        rows = rows_of(k)
        return pltpu.make_async_copy(tm_h.at[rows], g_next.at[rows], recv_sem.at[GUESS, k])

    @pl.when(n == count - 1)
    def _():
        each(lambda k, rows: terminal_copy(k).start())
        vc_next[...] = jnp.zeros_like(vc_next)

    @pl.when(n == count - 2)
    def _():
        wc_next[...] = jnp.zeros_like(wc_next)
        x_up[...] = jnp.zeros_like(x_up)

    @pl.when(n == count - 4)
    def _():
        x_next[...] = jnp.zeros_like(x_next)

    loads[0].wait()
    loads[1].wait()
    h = jnp.tanh(matmul(cp[...], wi[0]))
    act[0] = h.astype(BF)
    slope[0] = 1.0 - h * h
    loads[2].wait()
    state_one[...] = (cp[...].astype(F32) + matmul(act[0], wo[0])).astype(BF)
    loads[3].wait()
    h = jnp.tanh(matmul(state_one[...], wi[1]))
    act[1] = h.astype(BF)
    slope[1] = 1.0 - h * h
    loads[4].wait()
    for layer in (1, 0):
        wot[layer] = wo[layer].T
        wit[layer] = wi[layer].T
    loads[5].wait()

    @pl.when(even)
    def _core_zero():
        each(lambda k, rows: arrived(GUESS_IN, k, g_next))
        every = pl.ds(0, total)
        value = g_next[...]
        value = value + moved(value, 1, every)
        value = value + moved(value, 0, every)
        r1[...] = value - gs[...]

        def level_one(k, rows):
            arrived(R1, k, r1_next)
            value = r1_next[rows, :]
            vc[rows, :] = value + 2.0 * moved(value, 0, rows) + r1[rows, :]

            @pl.when(n >= 1)
            def _():
                message(VC, k, vc, vc_next, n - 1).start()

        each(level_one)

        def level_one_residual(k, rows):
            arrived(Y, k, y)
            value = y[rows, :]
            r2[rows, :] = value + 2.0 * moved(value, 0, rows)

            @pl.when(chip_odd)
            def _():
                message(R2, k, r2, r2_next, n - 2).start()

        each(level_one_residual)

        @pl.when(chip_even)
        def _even_chip():
            def level_two(k, rows):
                arrived(R2, k, r2_next)
                value = r2_next[rows, :]
                wc[rows, :] = value + 4.0 * moved(value, 0, rows) + r2[rows, :]

                @pl.when(n >= 2)
                def _():
                    message(WC, k, wc, wc_next, n - 2).start()

            each(level_two)

            def level_two_residual(k, rows):
                arrived(U, k, u)
                value = u[rows, :]
                r3[rows, :] = value + 4.0 * moved(value, 0, rows)

                @pl.when(pair_odd)
                def _():
                    message(R3, k, r3, r3_next, n - 4).start()

            each(level_two_residual)

            @pl.when(pair_even)
            def _():
                def level_three(k, rows):
                    arrived(R3, k, r3_next)
                    value = r3_next[rows, :]
                    x[rows, :] = value + 8.0 * moved(value, 0, rows) + r3[rows, :]

                    @pl.when(n >= 4)
                    def _():
                        message(X, k, x, x_next, n - 4).start()

                each(level_three)

                @pl.when(n >= 2)
                def _():
                    each(lambda k, rows: message(XUP, k, x, x_up, n - 2).start())

            @pl.when(pair_odd)
            def _():
                def level_three(k, rows):
                    @pl.when(n + 4 < count)
                    def _():
                        arrived(X, k, x_next)

                    value = x_next[rows, :]
                    x[rows, :] = value + 8.0 * moved(value, 0, rows) + r3[rows, :]
                    message(XUP, k, x, x_up, n - 2).start()

                each(level_three)

            w[...] = wc[...] + x[...]

        @pl.when(chip_odd)
        def _odd_chip():
            def level_two(k, rows):
                @pl.when(n + 2 < count)
                def _():
                    arrived(WC, k, wc_next)

                value = wc_next[rows, :]
                u_out = value + 4.0 * moved(value, 0, rows)
                wc[rows, :] = u_out
                message(U, k, wc, u, n - 2).start()

            each(level_two)

            def level_two_up(k, rows):
                @pl.when(n + 2 < count)
                def _():
                    arrived(XUP, k, x_up)

                value = wc_next[rows, :] + x_up[rows, :]
                w_next[rows, :] = value
                message(W_IN, k, w_next, w_above, n + 1, W).start()
                w[rows, :] = value + 4.0 * moved(value, 0, rows) + r2[rows, :]
                message(W, k, w, w_above, n - 1).start()

            each(level_two_up)

        adj[0] = gs[...] + (vc[...] + w[...])

        def fine(k, rows):
            arrived(E, k, e_next)
            value = e_next[rows, :]
            part = tangent(value, 1, rows)
            tang[1, rows, :] = part
            value = value + matmul(part, wit[1])
            adj[1, rows, :] = value
            tang[0, rows, :] = tangent(value, 0, rows)

        each(fine)

    @pl.when(jnp.logical_not(even))
    def _core_one():
        def fine_residual(k, rows):
            @pl.when(n + 1 < count)
            def _():
                arrived(GUESS, k, g_next)

            @pl.when(n + 1 == count)
            def _():
                terminal_copy(k).wait()

            value = g_next[rows, :]
            value = value + moved(value, 1, rows)
            value = value + moved(value, 0, rows)
            r1[rows, :] = value - gs[rows, :]
            message(R1, k, r1, r1_next, n - 1).start()

        each(fine_residual)

        def level_one(k, rows):
            @pl.when(n + 1 < count)
            def _():
                arrived(VC, k, vc_next)

            value = vc_next[rows, :]
            vc[rows, :] = value + 2.0 * moved(value, 0, rows)
            message(Y, k, vc, y, n - 1).start()

        each(level_one)

        def level_one_up(k, rows):
            arrived(W, k, w_above)
            value = vc_next[rows, :] + w_above[rows, :]
            e_next[rows, :] = g_next[rows, :] + value
            adj[0, rows, :] = gs[rows, :] + (value + 2.0 * moved(value, 0, rows) + r1[rows, :])
            message(E, k, adj.at[0], e_next, n - 1).start()

        each(level_one_up)

        every = pl.ds(0, total)
        value = e_next[...]
        part = tangent(value, 1, every)
        tang[1] = part
        value = value + matmul(part, wit[1])
        adj[1] = value
        tang[0] = tangent(value, 0, every)

    def transposed_dot(a, b):
        return lax.dot_general(a, b, (((0,), (0,)), ((), ())), preferred_element_type=F32)

    stores = [
        pltpu.make_async_copy(source, target, store_sem.at[place])
        for place, (source, target) in enumerate(
            (
                (adj, adj_h),
                (gi.at[1], gi_h.at[1]),
                (go.at[1], go_h.at[1]),
                (gi.at[0], gi_h.at[0]),
                (go.at[0], go_h.at[0]),
            )
        )
    ]
    stores[0].start()
    gi[1] = transposed_dot(state_one[...], tang[1]).astype(BF)
    stores[1].start()
    go[1] = transposed_dot(act[1], e_next[...].astype(BF)).astype(BF)
    stores[2].start()
    gi[0] = transposed_dot(cp[...], tang[0]).astype(BF)
    stores[3].start()
    go[0] = transposed_dot(act[0], adj[1].astype(BF)).astype(BF)
    stores[4].start()

    sent = (
        (GUESS_IN, jnp.logical_not(even)),
        (GUESS, jnp.logical_and(even, n >= 1)),
        (R1, jnp.logical_not(even)),
        (VC, jnp.logical_and(even, n >= 1)),
        (Y, jnp.logical_not(even)),
        (R2, chip_odd),
        (WC, jnp.logical_and(chip_even, n >= 2)),
        (U, chip_odd),
        (R3, pair_odd),
        (X, jnp.logical_and(pair_even, n >= 4)),
        (XUP, jnp.logical_and(chip_even, n >= 2)),
        (W_IN, chip_odd),
        (W, chip_odd),
        (E, jnp.logical_not(even)),
    )
    for kind, done in sent:

        @pl.when(done)
        def _(kind=kind):
            each(lambda k, rows: message(kind, k, r1, r1, n).wait_send())

    for copy in stores:
        copy.wait()


def local(w_in, w_out, checkpoint, guess, terminal, rows_per=32):
    count = lax.axis_size("depth")
    pair, width, hidden = w_in.shape
    rows = terminal.shape[0]
    chunks = rows // rows_per
    anywhere = pl.BlockSpec(memory_space=pl.ANY)
    plane = pltpu.VMEM((rows, width), F32)
    return pl.pallas_call(
        functools.partial(kernel, count, rows_per),
        out_shape=(
            jax.ShapeDtypeStruct((pair, rows, width), F32),
            jax.ShapeDtypeStruct((pair, width, hidden), BF),
            jax.ShapeDtypeStruct((pair, hidden, width), BF),
        ),
        in_specs=[anywhere] * 5,
        out_specs=(anywhere,) * 3,
        scratch_shapes=[
            pltpu.VMEM((pair, width, hidden), BF),
            pltpu.VMEM((pair, hidden, width), BF),
            pltpu.VMEM((pair, hidden, width), BF),
            pltpu.VMEM((pair, width, hidden), BF),
            pltpu.VMEM((rows, width), BF),
            plane,
            pltpu.VMEM((rows, width), BF),
            pltpu.VMEM((pair, rows, hidden), BF),
            pltpu.VMEM((pair, rows, hidden), F32),
            pltpu.VMEM((pair, rows, hidden), BF),
        ]
        + [plane] * 20
        + [
            pltpu.VMEM((pair, rows, width), F32),
            pltpu.VMEM((pair, width, hidden), BF),
            pltpu.VMEM((pair, hidden, width), BF),
            pltpu.SemaphoreType.DMA((6,)),
            pltpu.SemaphoreType.DMA((5,)),
            pltpu.SemaphoreType.DMA((MESSAGES, chunks)),
            pltpu.SemaphoreType.DMA((MESSAGES, chunks)),
        ],
        compiler_params=pltpu.CompilerParams(
            collective_id=0, has_side_effects=True, vmem_limit_bytes=56 << 20
        ),
        name="vcycle",
    )(w_in, w_out, checkpoint, guess, terminal)


def solution(mesh):
    split = P("depth", None, None)
    return jax.shard_map(
        local,
        mesh=mesh,
        in_specs=(split, split, split, split, P()),
        out_specs=(split, split, split),
        check_vma=False,
    )
```

time: 269 us -> 75.8 us (0.28)
  the two profiles are of different devices: /device:TPU:4 before, /device:TPU:24 now
where the time goes in v1:
time: 75.8 us; the launch traced here: 75.6 us
  Pallas kernels  68.9 us (91%)
  local copies, waits for them, and re-layouts  6.08 us (8%)
    pallas_call x1, Pallas kernels, local(): pl.pallas_call(functools.partial(kernel, count, rows_per), out_shape=(jax...  68.9 us
    unnamed x7, local copies, waits for them, and re-layouts  6.08 us

profile of v1, /device:TPU:24, one launch (start us, length us, event | category | flops | bytes accessed | tf_op | source)
XLA Modules:
  0.0 75.6 jit_solution(16255276628389583823)
XLA Ops:
  0.6 68.9 %vcycle.1 = (f32[2,256,512]{2,1,0:T(8,128)}, bf16[2,512,1024]{2,1,0:T(8,128)(2,1)}, bf16[2,1024,512]{2,1,0:T(8,128)(2,1)}) custom-call(bf16[2,512,1024]{2,1,0:T(8,128)(2,1)} %wi_h.1, bf16[2,1024,512]{2,1,0:T(8,128)(2,1)} %wo_h.1, bf16[1,256,512]{2,1,0:T(8,128)(2,1)} %cp_h.1, f32[1,256,512]{2,1,0:T(8,128)} %gs_h.1, f32[256,512]{1,0:T(8,128)} %tm_h.1), custom_call_target="tpu_custom_call" | custom-call | tf_op jit(solution)/shard_map/vcycle/pallas_call | solution.py:377
  69.6 0.0 copy-start.1
  69.6 2.4 %copy.11 = f32[2,256,512]{2,1,0:T(8,128)} copy(f32[2,256,512]{2,1,0:T(8,128)} %get-tuple-element.6) | data formatting | bytes 2097152
  72.0 0.0 copy-done.1
  72.0 0.0 copy-start
  72.0 1.3 %copy.12 = bf16[2,512,1024]{2,1,0:T(8,128)(2,1)} copy(bf16[2,512,1024]{2,1,0:T(8,128)(2,1)S(1)} %copy-done.1) | data formatting | bytes 4194304
  73.3 1.0 %copy-done = bf16[2,1024,512]{2,1,0:T(8,128)(2,1)S(1)} copy-done((bf16[2,1024,512]{2,1,0:T(8,128)(2,1)S(1)}, bf16[2,1024,512]{2,1,0:T(8,128)(2,1)}, u32[]{:S(2)}) %copy-start) | copy-done | bytes 2097176
  74.3 1.3 %copy.13 = bf16[2,1024,512]{2,1,0:T(8,128)(2,1)} copy(bf16[2,1024,512]{2,1,0:T(8,128)(2,1)S(1)} %copy-done) | data formatting | bytes 4194304
Async XLA Ops:
  69.6 2.4 %copy-start.1 = (bf16[2,512,1024]{2,1,0:T(8,128)(2,1)S(1)}, bf16[2,512,1024]{2,1,0:T(8,128)(2,1)}, u32[]{:S(2)}) copy-start(bf16[2,512,1024]{2,1,0:T(8,128)(2,1)} %get-tuple-element.7) | copy-start | bytes 6291460
  72.0 2.3 %copy-start = (bf16[2,1024,512]{2,1,0:T(8,128)(2,1)S(1)}, bf16[2,1024,512]{2,1,0:T(8,128)(2,1)}, u32[]{:S(2)}) copy-start(bf16[2,1024,512]{2,1,0:T(8,128)(2,1)} %get-tuple-element.8) | copy-start | bytes 6291460

commit v2 on v1

v2 whole, which is shorter than its diff:
```python
import functools

import jax
import jax.numpy as jnp
from jax import lax
from jax.experimental import pallas as pl
from jax.experimental.pallas import tpu as pltpu
from jax.sharding import PartitionSpec as P

MESH = pl.DeviceIdType.MESH
BF = jnp.bfloat16
F32 = jnp.float32

GUESS_IN, GUESS, R1, VC, R2, WC, U, R3, X, XUP, W, W_DOWN, E = range(13)
MESSAGES = 13
EVEN, ODD, OTHER = 0, 1, 2


def matmul(a, b):
    return jnp.dot(a, b, preferred_element_type=F32)


def kernel(
    count, rows_per, wi_h, wo_h, cp_h, gs_h, tm_h, tang, act, state, nexts, adj,
    wi, wo, wit, wot, wide_in, wide_out, gs, slope,
    g_next, r1, r1_next, vc, vc_next, r2, r2_next, wc, wc_next, u, u_own, r3, r3_next, x, x_next, x_up, w, w_next, w_down, e_next,
    load_sem, hand_send, hand_recv, send_sem, recv_sem,
):
    n = lax.axis_index("depth")
    core_zero = lax.rem(n, 2) == 0
    core_one = lax.rem(n, 2) == 1
    chip_even = lax.rem(n, 4) == 1
    chip_odd = lax.rem(n, 4) == 3
    pair_even = lax.rem(n, 8) == 1
    pair_odd = lax.rem(n, 8) == 5
    total = gs.shape[0]
    chunks = total // rows_per
    every = pl.ds(0, total)

    def rows_of(k, several=1):
        size = rows_per * several
        return pl.ds(pl.multiple_of(k * size, size), size)

    def message(kind, k, source, target, peer):
        rows = rows_of(k)
        return pltpu.make_async_remote_copy(
            src_ref=source.at[rows],
            dst_ref=target.at[rows],
            send_sem=send_sem.at[kind, k],
            recv_sem=recv_sem.at[kind, k],
            device_id=(peer,),
            device_id_type=MESH,
        )

    def arrived(kind, k, target):
        message(kind, k, target, target, n).wait_recv()

    def each(body, several=1):
        def step(k, carry):
            body(k, rows_of(k, several))
            return carry

        lax.fori_loop(0, chunks // several, step, 0)

    def tangent(value, layer, rows):
        return (matmul(value.astype(BF), wot[layer]) * slope[layer, rows, :]).astype(BF)

    def moved(value, layer, rows):
        return matmul(tangent(value, layer, rows), wit[layer])

    loads = [
        pltpu.make_async_copy(source, target, load_sem.at[place])
        for place, (source, target) in enumerate(
            (
                (wo_h.at[0], wo.at[0]),
                (wi_h.at[0], wi.at[0]),
                (cp_h.at[0], state.at[0]),
                (wi_h.at[1], wi.at[1]),
                (wo_h.at[1], wo.at[1]),
                (gs_h.at[0], gs),
            )
        )
    ]
    for copy in loads:
        copy.start()

    barrier = pltpu.get_barrier_semaphore()
    peers = (
        (n + 1, n + 1 < count),
        (n - 1, n >= 1),
        (n + 2, jnp.logical_and(core_one, n + 2 < count)),
        (n - 2, jnp.logical_and(core_one, n >= 2)),
        (n + 4, jnp.logical_and(chip_even, n + 4 < count)),
        (n - 4, jnp.logical_and(chip_even, n >= 4)),
    )
    for peer, there in peers:

        @pl.when(there)
        def _(peer=peer):
            pl.semaphore_signal(barrier, inc=1, device_id=(peer,), device_id_type=MESH)

    greeted = sum(jnp.where(there, 1, 0) for _, there in peers)
    pl.semaphore_wait(barrier, greeted)

    @pl.when(core_one)
    def _():
        each(lambda k, rows: message(GUESS_IN, k, gs_h.at[0], g_next, n - 1).start())

    @pl.when(jnp.logical_and(core_zero, n >= 1))
    def _():
        each(lambda k, rows: message(GUESS, k, gs_h.at[0], g_next, n - 1).start())

    def terminal_copy(k):
        rows = rows_of(k)
        return pltpu.make_async_copy(tm_h.at[rows], g_next.at[rows], recv_sem.at[GUESS, k])

    @pl.when(n == count - 1)
    def _():
        each(lambda k, rows: terminal_copy(k).start())
        vc_next[...] = jnp.zeros_like(vc_next)
        wc_next[...] = jnp.zeros_like(wc_next)
        x_up[...] = jnp.zeros_like(x_up)

    @pl.when(n == count - 3)
    def _():
        x_next[...] = jnp.zeros_like(x_next)

    def handed(place, source, target, peer):
        return pltpu.make_async_remote_copy(
            src_ref=source,
            dst_ref=target,
            send_sem=hand_send.at[place],
            recv_sem=hand_recv.at[place],
            device_id=(peer,),
            device_id_type=MESH,
        )

    def hand_out(peer):
        return handed(0, wide_out, wide_out, peer)

    def hand_in(peer):
        return handed(1, wide_in, wide_in, peer)

    def hand_slope(peer):
        return handed(2, slope.at[EVEN], slope.at[OTHER], peer)

    loads[0].wait()
    wot[EVEN] = wo[EVEN].T

    @pl.when(core_zero)
    def _():
        wide_out[...] = wot[EVEN].astype(F32)
        hand_out(n + 1).start()

    loads[1].wait()
    wit[EVEN] = wi[EVEN].T

    @pl.when(core_zero)
    def _():
        wide_in[...] = wit[EVEN].astype(F32)
        hand_in(n + 1).start()

    loads[2].wait()
    h = jnp.tanh(matmul(state[EVEN], wi[EVEN]))
    act[EVEN] = h.astype(BF)
    slope[EVEN] = 1.0 - h * h

    @pl.when(core_zero)
    def _():
        hand_slope(n + 1).start()

    state[ODD] = (state[EVEN].astype(F32) + matmul(act[EVEN], wo[EVEN])).astype(BF)
    loads[3].wait()
    h = jnp.tanh(matmul(state[ODD], wi[ODD]))
    act[ODD] = h.astype(BF)
    slope[ODD] = 1.0 - h * h
    loads[4].wait()
    wot[ODD] = wo[ODD].T
    wit[ODD] = wi[ODD].T
    loads[5].wait()

    @pl.when(core_zero)
    def _core_zero():
        each(lambda k, rows: arrived(GUESS_IN, k, g_next))
        value = g_next[...]
        value = value + moved(value, ODD, every)
        value = value + moved(value, EVEN, every)
        r1[...] = value - gs[...]

        def level_one(k, rows):
            arrived(R1, k, r1_next)
            value = r1_next[rows, :]
            vc[rows, :] = value + 2.0 * moved(value, EVEN, rows) + r1[rows, :]

            @pl.when(n >= 1)
            def _():
                message(VC, k, vc, vc_next, n - 1).start()

        each(level_one)
        each(lambda k, rows: arrived(W_DOWN, k, w_down))
        adj[EVEN] = gs[...] + (vc[...] + w_down[...])

        def fine(k, rows):
            arrived(E, k, e_next)
            value = e_next[rows, :]
            nexts[ODD, rows, :] = value.astype(BF)
            part = tangent(value, ODD, rows)
            tang[ODD, rows, :] = part
            value = value + matmul(part, wit[ODD])
            adj[ODD, rows, :] = value
            nexts[EVEN, rows, :] = value.astype(BF)
            tang[EVEN, rows, :] = tangent(value, EVEN, rows)

        each(fine)

    @pl.when(core_one)
    def _core_one():
        def fine_residual(pair, rows):
            for k in (2 * pair, 2 * pair + 1):

                @pl.when(n + 1 < count)
                def _(k=k):
                    arrived(GUESS, k, g_next)

                @pl.when(n + 1 == count)
                def _(k=k):
                    terminal_copy(k).wait()

            value = g_next[rows, :]
            value = value + moved(value, ODD, rows)
            value = value + moved(value, EVEN, rows)
            r1[rows, :] = value - gs[rows, :]
            for k in (2 * pair, 2 * pair + 1):
                message(R1, k, r1, r1_next, n - 1).start()

        each(fine_residual, 2)
        hand_out(n).wait_recv()
        wot[OTHER] = wide_out[...].astype(BF)
        hand_in(n).wait_recv()
        wit[OTHER] = wide_in[...].astype(BF)
        hand_slope(n).wait_recv()

        def level_one_residual(pair, rows):
            @pl.when(n + 1 < count)
            def _():
                for k in (2 * pair, 2 * pair + 1):
                    arrived(VC, k, vc_next)

            value = vc_next[rows, :]
            value = value + 2.0 * moved(value, EVEN, rows)
            r2[rows, :] = value + 2.0 * moved(value, OTHER, rows)

            @pl.when(chip_odd)
            def _():
                for k in (2 * pair, 2 * pair + 1):
                    message(R2, k, r2, r2_next, n - 2).start()

        each(level_one_residual, 2)

        @pl.when(chip_even)
        def _even_chip():
            def level_two(k, rows):
                arrived(R2, k, r2_next)
                value = r2_next[rows, :]
                wc[rows, :] = value + 4.0 * moved(value, OTHER, rows) + r2[rows, :]

                @pl.when(n >= 2)
                def _():
                    message(WC, k, wc, wc_next, n - 2).start()

            each(level_two)

            def level_two_residual(k, rows):
                arrived(U, k, u)
                value = u[rows, :]
                r3[rows, :] = value + 4.0 * moved(value, OTHER, rows)

                @pl.when(pair_odd)
                def _():
                    message(R3, k, r3, r3_next, n - 4).start()

            each(level_two_residual)

            @pl.when(pair_even)
            def _():
                def level_three(k, rows):
                    arrived(R3, k, r3_next)
                    value = r3_next[rows, :]
                    x[rows, :] = value + 8.0 * moved(value, OTHER, rows) + r3[rows, :]

                    @pl.when(n >= 4)
                    def _():
                        message(X, k, x, x_next, n - 4).start()

                each(level_three)

                @pl.when(n >= 2)
                def _():
                    each(lambda k, rows: message(XUP, k, x, x_up, n - 2).start())

            @pl.when(pair_odd)
            def _():
                def level_three(k, rows):
                    @pl.when(n + 4 < count)
                    def _():
                        arrived(X, k, x_next)

                    value = x_next[rows, :]
                    x[rows, :] = value + 8.0 * moved(value, OTHER, rows) + r3[rows, :]
                    message(XUP, k, x, x_up, n - 2).start()

                each(level_three)

            w[...] = wc[...] + x[...]

        @pl.when(chip_odd)
        def _odd_chip():
            def level_two(k, rows):
                @pl.when(n + 2 < count)
                def _():
                    arrived(WC, k, wc_next)

                value = wc_next[rows, :]
                u_own[rows, :] = value + 4.0 * moved(value, OTHER, rows)
                message(U, k, u_own, u, n - 2).start()

            each(level_two)

            def level_two_up(k, rows):
                @pl.when(n + 2 < count)
                def _():
                    arrived(XUP, k, x_up)

                value = wc_next[rows, :] + x_up[rows, :]
                w_next[rows, :] = value
                w[rows, :] = value + 4.0 * moved(value, OTHER, rows) + r2[rows, :]
                message(W, k, w, w_next, n - 2).start()

            each(level_two_up)

        each(lambda k, rows: message(W_DOWN, k, w, w_down, n - 1).start())

        def level_one_up(k, rows):
            @pl.when(chip_even)
            def _():
                arrived(W, k, w_next)

            value = vc_next[rows, :] + w_next[rows, :]
            e_next[rows, :] = g_next[rows, :] + value
            adj[EVEN, rows, :] = gs[rows, :] + (value + 2.0 * moved(value, EVEN, rows) + r1[rows, :])
            message(E, k, adj.at[EVEN], e_next, n - 1).start()

        each(level_one_up)
        value = e_next[...]
        nexts[ODD] = value.astype(BF)
        part = tangent(value, ODD, every)
        tang[ODD] = part
        value = value + matmul(part, wit[ODD])
        adj[ODD] = value
        nexts[EVEN] = value.astype(BF)
        tang[EVEN] = tangent(value, EVEN, every)

    sent = (
        (GUESS_IN, core_one),
        (GUESS, jnp.logical_and(core_zero, n >= 1)),
        (R1, core_one),
        (VC, jnp.logical_and(core_zero, n >= 1)),
        (R2, chip_odd),
        (WC, jnp.logical_and(chip_even, n >= 2)),
        (U, chip_odd),
        (R3, pair_odd),
        (X, jnp.logical_and(pair_even, n >= 4)),
        (XUP, jnp.logical_and(chip_even, n >= 2)),
        (W, chip_odd),
        (W_DOWN, core_one),
        (E, core_one),
    )
    for kind, done in sent:

        @pl.when(done)
        def _(kind=kind):
            each(lambda k, rows: message(kind, k, r1, r1, n).wait_send())

    @pl.when(core_zero)
    def _():
        hand_out(n).wait_send()
        hand_in(n).wait_send()
        hand_slope(n).wait_send()


def gradients(tang, act, state, nexts, adj, adj_h, gi_h, go_h, gi, go, store_sem):
    def transposed_dot(a, b):
        return lax.dot_general(a, b, (((0,), (0,)), ((), ())), preferred_element_type=F32)

    stores = [
        pltpu.make_async_copy(source, target, store_sem.at[place])
        for place, (source, target) in enumerate(
            (
                (adj, adj_h),
                (gi.at[0], gi_h.at[0]),
                (go.at[0], go_h.at[0]),
                (gi.at[1], gi_h.at[1]),
                (go.at[1], go_h.at[1]),
            )
        )
    ]
    stores[0].start()
    for layer in (0, 1):
        gi[layer] = transposed_dot(state[layer], tang[layer]).astype(BF)
        stores[1 + 2 * layer].start()
        go[layer] = transposed_dot(act[layer], nexts[layer]).astype(BF)
        stores[2 + 2 * layer].start()
    for copy in stores:
        copy.wait()


def local(w_in, w_out, checkpoint, guess, terminal, rows_per=64):
    count = lax.axis_size("depth")
    pair, width, hidden = w_in.shape
    rows = terminal.shape[0]
    chunks = rows // rows_per
    anywhere = pl.BlockSpec(memory_space=pltpu.HBM)
    inside = pl.BlockSpec(memory_space=pltpu.VMEM)
    plane = pltpu.VMEM((rows, width), F32)
    kept = pl.pallas_call(
        functools.partial(kernel, count, rows_per),
        out_shape=(
            pltpu.VMEM((pair, rows, hidden), BF),
            pltpu.VMEM((pair, rows, hidden), BF),
            pltpu.VMEM((pair, rows, width), BF),
            pltpu.VMEM((pair, rows, width), BF),
            pltpu.VMEM((pair, rows, width), F32),
        ),
        in_specs=[anywhere] * 5,
        out_specs=(inside,) * 5,
        scratch_shapes=[
            pltpu.VMEM((pair, width, hidden), BF),
            pltpu.VMEM((pair, hidden, width), BF),
            pltpu.VMEM((pair + 1, hidden, width), BF),
            pltpu.VMEM((pair + 1, width, hidden), BF),
            pltpu.VMEM((hidden, width), F32),
            pltpu.VMEM((width, hidden), F32),
            plane,
            pltpu.VMEM((pair + 1, rows, hidden), F32),
        ]
        + [plane] * 20
        + [
            pltpu.SemaphoreType.DMA((6,)),
            pltpu.SemaphoreType.DMA((3,)),
            pltpu.SemaphoreType.DMA((3,)),
            pltpu.SemaphoreType.DMA((MESSAGES, chunks)),
            pltpu.SemaphoreType.DMA((MESSAGES, chunks)),
        ],
        compiler_params=pltpu.CompilerParams(
            collective_id=0, has_side_effects=True, vmem_limit_bytes=44 << 20
        ),
        name="vcycle",
    )(*(pltpu.with_memory_space_constraint(a, pltpu.HBM) for a in (w_in, w_out, checkpoint, guess, terminal)))
    return pl.pallas_call(
        gradients,
        out_shape=(
            jax.ShapeDtypeStruct((pair, rows, width), F32),
            jax.ShapeDtypeStruct((pair, width, hidden), BF),
            jax.ShapeDtypeStruct((pair, hidden, width), BF),
        ),
        in_specs=[inside] * 5,
        out_specs=(anywhere,) * 3,
        scratch_shapes=[
            pltpu.VMEM((pair, width, hidden), BF),
            pltpu.VMEM((pair, hidden, width), BF),
            pltpu.SemaphoreType.DMA((5,)),
        ],
        compiler_params=pltpu.CompilerParams(vmem_limit_bytes=24 << 20),
        name="gradients",
    )(*kept)


def solution(mesh):
    split = P("depth", None, None)
    return jax.shard_map(
        local,
        mesh=mesh,
        in_specs=(split, split, split, split, P()),
        out_specs=(split, split, split),
        check_vma=False,
    )
```

time: 75.8 us -> 67.5 us (0.89)
  local copies, waits for them, and re-layouts: 6.08 us -> 0 us
  Pallas kernels: 68.9 us -> 66.8 us
    unnamed x7 -> x0, local copies, waits for them, and re-layouts: 6.08 us -> none
    pallas_call x1 -> x2, Pallas kernels: 68.9 us -> 66.8 us  [the longest x1 64.3 us: local(): pl.pallas_call(functools.partial(kernel, count, rows_per), out_shape=(plt...]
where the time goes in v2:
time: 67.5 us; the launch traced here: 67.4 us
  Pallas kernels  66.8 us (99%)
    pallas_call x1, Pallas kernels, local(): pl.pallas_call(functools.partial(kernel, count, rows_per), out_shape=(plt...  64.3 us
    pallas_call x1, Pallas kernels, local(): pl.pallas_call(gradients, out_shape=(jax.ShapeDtypeStruct((pair, rows, wi...  2.51 us

profile of v2, /device:TPU:24, one launch (start us, length us, event | category | flops | bytes accessed | tf_op | source)
XLA Modules:
  0.0 67.4 jit_solution(17054400843499937139)
XLA Ops:
  0.6 64.3 %vcycle.1 = (bf16[2,256,1024]{2,1,0:T(8,128)(2,1)S(1)}, bf16[2,256,1024]{2,1,0:T(8,128)(2,1)S(1)}, bf16[2,256,512]{2,1,0:T(8,128)(2,1)S(1)}, bf16[2,256,512]{2,1,0:T(8,128)(2,1)S(1)}, f32[2,256,512]{2,1,0:T(8,128)S(1)}) custom-call(bf16[2,512,1024]{2,1,0:T(8,128)(2,1)} %wi_h.1, bf16[2,1024,512]{2,1,0:T(8,128)(2,1)} %wo_h.1, bf16[1,256,512]{2,1,0:T(8,128)(2,1)} %cp_h.1, ...), custom_call_target="tpu_custom_call" | custom-call | tf_op jit(solution)/shard_map/vcycle/pallas_call | solution.py:425
  64.9 2.5 %gradients.1 = (f32[2,256,512]{2,1,0:T(8,128)}, bf16[2,512,1024]{2,1,0:T(8,128)(2,1)}, bf16[2,1024,512]{2,1,0:T(8,128)(2,1)}) custom-call(bf16[2,256,1024]{2,1,0:T(8,128)(2,1)S(1)} %get-tuple-element.8.tang, bf16[2,256,1024]{2,1,0:T(8,128)(2,1)S(1)} %get-tuple-element.9.act, bf16[2,256,512]{2,1,0:T(8,128)(2,1)S(1)} %get-tuple-element.10.state, ...), custom_call_target="tpu_custom_call" | custom-call | tf_op jit(solution)/shard_map/gradients/pallas_call | solution.py:459

commit v3 on v2

--- a/solution.py
+++ b/solution.py
@@ -62,6 +62,37 @@
 
         lax.fori_loop(0, chunks // several, step, 0)
 
+    def interleaved(first, second, lag=2):
+        def step(k, carry):
+            @pl.when(k < chunks)
+            def _():
+                first(k, rows_of(k))
+
+            @pl.when(k >= lag)
+            def _():
+                second(k - lag, rows_of(k - lag))
+
+            return carry
+
+        lax.fori_loop(0, chunks + lag, step, 0)
+
+    def down(peer):
+        return pltpu.make_async_remote_copy(
+            src_ref=w,
+            dst_ref=w_down,
+            send_sem=send_sem.at[W_DOWN, 0],
+            recv_sem=recv_sem.at[W_DOWN, 0],
+            device_id=(peer,),
+            device_id_type=MESH,
+        )
+
+    def settle(*sent):
+        for kind, done in sent:
+
+            @pl.when(done)
+            def _(kind=kind):
+                each(lambda k, rows: message(kind, k, r1, r1, n).wait_send())
+
     def tangent(value, layer, rows):
         return (matmul(value.astype(BF), wot[layer]) * slope[layer, rows, :]).astype(BF)
 
@@ -124,6 +155,9 @@
     @pl.when(n == count - 3)
     def _():
         x_next[...] = jnp.zeros_like(x_next)
+        r2_next[...] = jnp.zeros_like(r2_next)
+        u[...] = jnp.zeros_like(u)
+        w_next[...] = jnp.zeros_like(w_next)
 
     def handed(place, source, target, peer):
         return pltpu.make_async_remote_copy(
@@ -197,7 +231,11 @@
                 message(VC, k, vc, vc_next, n - 1).start()
 
         each(level_one)
-        each(lambda k, rows: arrived(W_DOWN, k, w_down))
+        settle((GUESS, n >= 1), (VC, n >= 1))
+        hand_out(n).wait_send()
+        hand_in(n).wait_send()
+        hand_slope(n).wait_send()
+        down(n).wait_recv()
         adj[EVEN] = gs[...] + (vc[...] + w_down[...])
 
         def fine(k, rows):
@@ -215,52 +253,50 @@
 
     @pl.when(core_one)
     def _core_one():
-        def fine_residual(pair, rows):
-            for k in (2 * pair, 2 * pair + 1):
-
-                @pl.when(n + 1 < count)
-                def _(k=k):
-                    arrived(GUESS, k, g_next)
-
-                @pl.when(n + 1 == count)
-                def _(k=k):
-                    terminal_copy(k).wait()
+        def fine_residual(k, rows):
+            @pl.when(n + 1 < count)
+            def _():
+                arrived(GUESS, k, g_next)
+
+            @pl.when(n + 1 == count)
+            def _():
+                terminal_copy(k).wait()
 
             value = g_next[rows, :]
             value = value + moved(value, ODD, rows)
             value = value + moved(value, EVEN, rows)
             r1[rows, :] = value - gs[rows, :]
-            for k in (2 * pair, 2 * pair + 1):
-                message(R1, k, r1, r1_next, n - 1).start()
-
-        each(fine_residual, 2)
+            message(R1, k, r1, r1_next, n - 1).start()
+
+        each(fine_residual)
         hand_out(n).wait_recv()
         wot[OTHER] = wide_out[...].astype(BF)
         hand_in(n).wait_recv()
         wit[OTHER] = wide_in[...].astype(BF)
         hand_slope(n).wait_recv()
-
-        def level_one_residual(pair, rows):
+        passes = jnp.logical_and(chip_odd, n + 1 < count)
+        hears = n + 3 < count
+
+        def level_one_residual(k, rows):
             @pl.when(n + 1 < count)
             def _():
-                for k in (2 * pair, 2 * pair + 1):
-                    arrived(VC, k, vc_next)
+                arrived(VC, k, vc_next)
 
             value = vc_next[rows, :]
             value = value + 2.0 * moved(value, EVEN, rows)
             r2[rows, :] = value + 2.0 * moved(value, OTHER, rows)
 
-            @pl.when(chip_odd)
-            def _():
-                for k in (2 * pair, 2 * pair + 1):
-                    message(R2, k, r2, r2_next, n - 2).start()
-
-        each(level_one_residual, 2)
+            @pl.when(passes)
+            def _():
+                message(R2, k, r2, r2_next, n - 2).start()
 
         @pl.when(chip_even)
         def _even_chip():
             def level_two(k, rows):
-                arrived(R2, k, r2_next)
+                @pl.when(hears)
+                def _():
+                    arrived(R2, k, r2_next)
+
                 value = r2_next[rows, :]
                 wc[rows, :] = value + 4.0 * moved(value, OTHER, rows) + r2[rows, :]
 
@@ -268,18 +304,19 @@
                 def _():
                     message(WC, k, wc, wc_next, n - 2).start()
 
-            each(level_two)
+            interleaved(level_one_residual, level_two)
 
             def level_two_residual(k, rows):
-                arrived(U, k, u)
+                @pl.when(hears)
+                def _():
+                    arrived(U, k, u)
+
                 value = u[rows, :]
                 r3[rows, :] = value + 4.0 * moved(value, OTHER, rows)
 
                 @pl.when(pair_odd)
                 def _():
                     message(R3, k, r3, r3_next, n - 4).start()
-
-            each(level_two_residual)
 
             @pl.when(pair_even)
             def _():
@@ -292,7 +329,7 @@
                     def _():
                         message(X, k, x, x_next, n - 4).start()
 
-                each(level_three)
+                interleaved(level_two_residual, level_three)
 
                 @pl.when(n >= 2)
                 def _():
@@ -300,6 +337,8 @@
 
             @pl.when(pair_odd)
             def _():
+                each(level_two_residual)
+
                 def level_three(k, rows):
                     @pl.when(n + 4 < count)
                     def _():
@@ -315,33 +354,50 @@
 
         @pl.when(chip_odd)
         def _odd_chip():
+            each(level_one_residual)
+
             def level_two(k, rows):
-                @pl.when(n + 2 < count)
+                @pl.when(n + 1 < count)
                 def _():
                     arrived(WC, k, wc_next)
 
                 value = wc_next[rows, :]
                 u_own[rows, :] = value + 4.0 * moved(value, OTHER, rows)
-                message(U, k, u_own, u, n - 2).start()
+
+                @pl.when(passes)
+                def _():
+                    message(U, k, u_own, u, n - 2).start()
 
             each(level_two)
 
             def level_two_up(k, rows):
-                @pl.when(n + 2 < count)
+                @pl.when(n + 1 < count)
                 def _():
                     arrived(XUP, k, x_up)
 
                 value = wc_next[rows, :] + x_up[rows, :]
                 w_next[rows, :] = value
                 w[rows, :] = value + 4.0 * moved(value, OTHER, rows) + r2[rows, :]
-                message(W, k, w, w_next, n - 2).start()
+
+                @pl.when(passes)
+                def _():
+                    message(W, k, w, w_next, n - 2).start()
 
             each(level_two_up)
 
-        each(lambda k, rows: message(W_DOWN, k, w, w_down, n - 1).start())
+        down(n - 1).start()
+        settle(
+            (GUESS_IN, core_one),
+            (R1, core_one),
+            (R2, passes),
+            (WC, jnp.logical_and(chip_even, n >= 2)),
+            (U, passes),
+            (R3, pair_odd),
+            (X, jnp.logical_and(pair_even, n >= 4)),
+        )
 
         def level_one_up(k, rows):
-            @pl.when(chip_even)
+            @pl.when(jnp.logical_and(chip_even, hears))
             def _():
                 arrived(W, k, w_next)
 
@@ -359,33 +415,8 @@
         adj[ODD] = value
         nexts[EVEN] = value.astype(BF)
         tang[EVEN] = tangent(value, EVEN, every)
-
-    sent = (
-        (GUESS_IN, core_one),
-        (GUESS, jnp.logical_and(core_zero, n >= 1)),
-        (R1, core_one),
-        (VC, jnp.logical_and(core_zero, n >= 1)),
-        (R2, chip_odd),
-        (WC, jnp.logical_and(chip_even, n >= 2)),
-        (U, chip_odd),
-        (R3, pair_odd),
-        (X, jnp.logical_and(pair_even, n >= 4)),
-        (XUP, jnp.logical_and(chip_even, n >= 2)),
-        (W, chip_odd),
-        (W_DOWN, core_one),
-        (E, core_one),
-    )
-    for kind, done in sent:
-
-        @pl.when(done)
-        def _(kind=kind):
-            each(lambda k, rows: message(kind, k, r1, r1, n).wait_send())
-
-    @pl.when(core_zero)
-    def _():
-        hand_out(n).wait_send()
-        hand_in(n).wait_send()
-        hand_slope(n).wait_send()
+        settle((XUP, jnp.logical_and(chip_even, n >= 2)), (W, passes), (E, core_one))
+        down(n).wait_send()
 
 
 def gradients(tang, act, state, nexts, adj, adj_h, gi_h, go_h, gi, go, store_sem):

time: 67.5 us -> 63.3 us (0.938)
  Pallas kernels: 66.8 us -> 62.5 us
    pallas_call x1, Pallas kernels: 64.3 us -> 60 us  [local(): pl.pallas_call(functools.partial(kernel, count, rows_per), out_shape=(plt...]
where the time goes in v3:
time: 63.3 us; the launch traced here: 63.2 us
  Pallas kernels  62.5 us (99%)
  between operations  0.64 us (1%)
    pallas_call x1, Pallas kernels, local(): pl.pallas_call(functools.partial(kernel, count, rows_per), out_shape=(plt...  60 us
    pallas_call x1, Pallas kernels, local(): pl.pallas_call(gradients, out_shape=(jax.ShapeDtypeStruct((pair, rows, wi...  2.51 us

profile of v3, /device:TPU:24, one launch (start us, length us, event | category | flops | bytes accessed | tf_op | source)
XLA Modules:
  0.0 63.2 jit_solution(15897005029474408537)
XLA Ops:
  0.6 60.0 %vcycle.1 = (bf16[2,256,1024]{2,1,0:T(8,128)(2,1)S(1)}, bf16[2,256,1024]{2,1,0:T(8,128)(2,1)S(1)}, bf16[2,256,512]{2,1,0:T(8,128)(2,1)S(1)}, bf16[2,256,512]{2,1,0:T(8,128)(2,1)S(1)}, f32[2,256,512]{2,1,0:T(8,128)S(1)}) custom-call(bf16[2,512,1024]{2,1,0:T(8,128)(2,1)} %wi_h.1, bf16[2,1024,512]{2,1,0:T(8,128)(2,1)} %wo_h.1, bf16[1,256,512]{2,1,0:T(8,128)(2,1)} %cp_h.1, ...), custom_call_target="tpu_custom_call" | custom-call | tf_op jit(solution)/shard_map/vcycle/pallas_call | solution.py:456
  60.7 2.5 %gradients.1 = (f32[2,256,512]{2,1,0:T(8,128)}, bf16[2,512,1024]{2,1,0:T(8,128)(2,1)}, bf16[2,1024,512]{2,1,0:T(8,128)(2,1)}) custom-call(bf16[2,256,1024]{2,1,0:T(8,128)(2,1)S(1)} %get-tuple-element.8.tang, bf16[2,256,1024]{2,1,0:T(8,128)(2,1)S(1)} %get-tuple-element.9.act, bf16[2,256,512]{2,1,0:T(8,128)(2,1)S(1)} %get-tuple-element.10.state, ...), custom_call_target="tpu_custom_call" | custom-call | tf_op jit(solution)/shard_map/gradients/pallas_call | solution.py:490

commit v4 on v3

--- a/solution.py
+++ b/solution.py
@@ -11,8 +11,11 @@
 BF = jnp.bfloat16
 F32 = jnp.float32
 
-GUESS_IN, GUESS, R1, VC, R2, WC, U, R3, X, XUP, W, W_DOWN, E = range(13)
-MESSAGES = 13
+GUESS_IN, GUESS, R1, VC, R2, WC, U, R3, X, XUP, X_BACK, W, W_DOWN, E = range(14)
+MESSAGES = 14
+FEW, MANY = 4, 8
+PIECES = {kind: MANY if kind in (R2, WC, U, R3, X, XUP, X_BACK, W) else FEW for kind in range(MESSAGES)}
+LAG_TWO, LAG_THREE = 1, 2
 EVEN, ODD, OTHER = 0, 1, 2
 
 
@@ -21,7 +24,7 @@
 
 
 def kernel(
-    count, rows_per, wi_h, wo_h, cp_h, gs_h, tm_h, tang, act, state, nexts, adj,
+    count, wi_h, wo_h, cp_h, gs_h, tm_h, tang, act, state, nexts, adj,
     wi, wo, wit, wot, wide_in, wide_out, gs, slope,
     g_next, r1, r1_next, vc, vc_next, r2, r2_next, wc, wc_next, u, u_own, r3, r3_next, x, x_next, x_up, w, w_next, w_down, e_next,
     load_sem, hand_send, hand_recv, send_sem, recv_sem,
@@ -34,47 +37,55 @@
     pair_even = lax.rem(n, 8) == 1
     pair_odd = lax.rem(n, 8) == 5
     total = gs.shape[0]
-    chunks = total // rows_per
     every = pl.ds(0, total)
 
-    def rows_of(k, several=1):
-        size = rows_per * several
+    def rows_of(k, pieces):
+        size = total // pieces
         return pl.ds(pl.multiple_of(k * size, size), size)
 
-    def message(kind, k, source, target, peer):
-        rows = rows_of(k)
+    def message(kind, k, source, target, peer, receives=None):
+        rows = rows_of(k, PIECES[kind])
         return pltpu.make_async_remote_copy(
             src_ref=source.at[rows],
             dst_ref=target.at[rows],
             send_sem=send_sem.at[kind, k],
-            recv_sem=recv_sem.at[kind, k],
+            recv_sem=recv_sem.at[kind if receives is None else receives, k],
             device_id=(peer,),
             device_id_type=MESH,
         )
 
-    def arrived(kind, k, target):
-        message(kind, k, target, target, n).wait_recv()
-
-    def each(body, several=1):
+    def send(kind, k, pieces, source, target, peer, receives=None):
+        each_has = PIECES[kind] // pieces
+        for i in range(each_has):
+            message(kind, k * each_has + i, source, target, peer, receives).start()
+
+    def arrived(kind, k, pieces, target):
+        each_has = PIECES[kind] // pieces
+        for i in range(each_has):
+            message(kind, k * each_has + i, target, target, n).wait_recv()
+
+    def each(body, pieces):
         def step(k, carry):
-            body(k, rows_of(k, several))
+            body(k, rows_of(k, pieces))
             return carry
 
-        lax.fori_loop(0, chunks // several, step, 0)
-
-    def interleaved(first, second, lag=2):
+        lax.fori_loop(0, pieces, step, 0)
+
+    def interleaved(first, few, second, many, lag):
         def step(k, carry):
-            @pl.when(k < chunks)
-            def _():
-                first(k, rows_of(k))
+            @pl.when(k < few)
+            def _():
+                first(k, rows_of(k, few))
 
             @pl.when(k >= lag)
             def _():
-                second(k - lag, rows_of(k - lag))
+                for i in range(many // few):
+                    place = (k - lag) * (many // few) + i
+                    second(place, rows_of(place, many))
 
             return carry
 
-        lax.fori_loop(0, chunks + lag, step, 0)
+        lax.fori_loop(0, few + lag, step, 0)
 
     def down(peer):
         return pltpu.make_async_remote_copy(
@@ -91,7 +102,7 @@
 
             @pl.when(done)
             def _(kind=kind):
-                each(lambda k, rows: message(kind, k, r1, r1, n).wait_send())
+                each(lambda k, rows: message(kind, k, r1, r1, n).wait_send(), PIECES[kind])
 
     def tangent(value, layer, rows):
         return (matmul(value.astype(BF), wot[layer]) * slope[layer, rows, :]).astype(BF)
@@ -135,19 +146,19 @@
 
     @pl.when(core_one)
     def _():
-        each(lambda k, rows: message(GUESS_IN, k, gs_h.at[0], g_next, n - 1).start())
+        each(lambda k, rows: send(GUESS_IN, k, FEW, gs_h.at[0], g_next, n - 1), FEW)
 
     @pl.when(jnp.logical_and(core_zero, n >= 1))
     def _():
-        each(lambda k, rows: message(GUESS, k, gs_h.at[0], g_next, n - 1).start())
+        each(lambda k, rows: send(GUESS, k, FEW, gs_h.at[0], g_next, n - 1), FEW)
 
     def terminal_copy(k):
-        rows = rows_of(k)
+        rows = rows_of(k, FEW)
         return pltpu.make_async_copy(tm_h.at[rows], g_next.at[rows], recv_sem.at[GUESS, k])
 
     @pl.when(n == count - 1)
     def _():
-        each(lambda k, rows: terminal_copy(k).start())
+        each(lambda k, rows: terminal_copy(k).start(), FEW)
         vc_next[...] = jnp.zeros_like(vc_next)
         wc_next[...] = jnp.zeros_like(wc_next)
         x_up[...] = jnp.zeros_like(x_up)
@@ -215,22 +226,22 @@
 
     @pl.when(core_zero)
     def _core_zero():
-        each(lambda k, rows: arrived(GUESS_IN, k, g_next))
+        each(lambda k, rows: arrived(GUESS_IN, k, FEW, g_next), FEW)
         value = g_next[...]
         value = value + moved(value, ODD, every)
         value = value + moved(value, EVEN, every)
         r1[...] = value - gs[...]
 
         def level_one(k, rows):
-            arrived(R1, k, r1_next)
+            arrived(R1, k, FEW, r1_next)
             value = r1_next[rows, :]
             vc[rows, :] = value + 2.0 * moved(value, EVEN, rows) + r1[rows, :]
 
             @pl.when(n >= 1)
             def _():
-                message(VC, k, vc, vc_next, n - 1).start()
-
-        each(level_one)
+                send(VC, k, FEW, vc, vc_next, n - 1)
+
+        each(level_one, FEW)
         settle((GUESS, n >= 1), (VC, n >= 1))
         hand_out(n).wait_send()
         hand_in(n).wait_send()
@@ -239,7 +250,7 @@
         adj[EVEN] = gs[...] + (vc[...] + w_down[...])
 
         def fine(k, rows):
-            arrived(E, k, e_next)
+            arrived(E, k, FEW, e_next)
             value = e_next[rows, :]
             nexts[ODD, rows, :] = value.astype(BF)
             part = tangent(value, ODD, rows)
@@ -249,14 +260,14 @@
             nexts[EVEN, rows, :] = value.astype(BF)
             tang[EVEN, rows, :] = tangent(value, EVEN, rows)
 
-        each(fine)
+        each(fine, FEW)
 
     @pl.when(core_one)
     def _core_one():
         def fine_residual(k, rows):
             @pl.when(n + 1 < count)
             def _():
-                arrived(GUESS, k, g_next)
+                arrived(GUESS, k, FEW, g_next)
 
             @pl.when(n + 1 == count)
             def _():
@@ -266,9 +277,9 @@
             value = value + moved(value, ODD, rows)
             value = value + moved(value, EVEN, rows)
             r1[rows, :] = value - gs[rows, :]
-            message(R1, k, r1, r1_next, n - 1).start()
-
-        each(fine_residual)
+            send(R1, k, FEW, r1, r1_next, n - 1)
+
+        each(fine_residual, FEW)
         hand_out(n).wait_recv()
         wot[OTHER] = wide_out[...].astype(BF)
         hand_in(n).wait_recv()
@@ -280,7 +291,7 @@
         def level_one_residual(k, rows):
             @pl.when(n + 1 < count)
             def _():
-                arrived(VC, k, vc_next)
+                arrived(VC, k, FEW, vc_next)
 
             value = vc_next[rows, :]
             value = value + 2.0 * moved(value, EVEN, rows)
@@ -288,92 +299,89 @@
 
             @pl.when(passes)
             def _():
-                message(R2, k, r2, r2_next, n - 2).start()
+                send(R2, k, FEW, r2, r2_next, n - 2)
 
         @pl.when(chip_even)
         def _even_chip():
             def level_two(k, rows):
                 @pl.when(hears)
                 def _():
-                    arrived(R2, k, r2_next)
+                    arrived(R2, k, MANY, r2_next)
 
                 value = r2_next[rows, :]
                 wc[rows, :] = value + 4.0 * moved(value, OTHER, rows) + r2[rows, :]
 
                 @pl.when(n >= 2)
                 def _():
-                    message(WC, k, wc, wc_next, n - 2).start()
-
-            interleaved(level_one_residual, level_two)
+                    send(WC, k, MANY, wc, wc_next, n - 2)
+
+            interleaved(level_one_residual, FEW, level_two, MANY, LAG_TWO)
 
             def level_two_residual(k, rows):
                 @pl.when(hears)
                 def _():
-                    arrived(U, k, u)
+                    arrived(U, k, MANY, u)
 
                 value = u[rows, :]
                 r3[rows, :] = value + 4.0 * moved(value, OTHER, rows)
 
                 @pl.when(pair_odd)
                 def _():
-                    message(R3, k, r3, r3_next, n - 4).start()
+                    send(R3, k, MANY, r3, r3_next, n - 4)
 
             @pl.when(pair_even)
             def _():
                 def level_three(k, rows):
-                    arrived(R3, k, r3_next)
+                    arrived(R3, k, MANY, r3_next)
                     value = r3_next[rows, :]
                     x[rows, :] = value + 8.0 * moved(value, OTHER, rows) + r3[rows, :]
 
                     @pl.when(n >= 4)
                     def _():
-                        message(X, k, x, x_next, n - 4).start()
-
-                interleaved(level_two_residual, level_three)
-
-                @pl.when(n >= 2)
-                def _():
-                    each(lambda k, rows: message(XUP, k, x, x_up, n - 2).start())
+                        send(X, k, MANY, x, x_next, n - 4)
+
+                interleaved(level_two_residual, MANY, level_three, MANY, LAG_THREE)
 
             @pl.when(pair_odd)
             def _():
-                each(level_two_residual)
+                each(level_two_residual, MANY)
 
                 def level_three(k, rows):
                     @pl.when(n + 4 < count)
                     def _():
-                        arrived(X, k, x_next)
+                        arrived(X, k, MANY, x_next)
+                        send(X_BACK, k, MANY, x_next, x_up, n + 2, XUP)
 
                     value = x_next[rows, :]
                     x[rows, :] = value + 8.0 * moved(value, OTHER, rows) + r3[rows, :]
-                    message(XUP, k, x, x_up, n - 2).start()
-
-                each(level_three)
+                    send(XUP, k, MANY, x, x_up, n - 2)
+
+                each(level_three, MANY)
 
             w[...] = wc[...] + x[...]
 
         @pl.when(chip_odd)
         def _odd_chip():
-            each(level_one_residual)
+            each(level_one_residual, FEW)
 
             def level_two(k, rows):
                 @pl.when(n + 1 < count)
                 def _():
-                    arrived(WC, k, wc_next)
+                    arrived(WC, k, MANY, wc_next)
 
                 value = wc_next[rows, :]
                 u_own[rows, :] = value + 4.0 * moved(value, OTHER, rows)
 
                 @pl.when(passes)
                 def _():
-                    message(U, k, u_own, u, n - 2).start()
-
-            each(level_two)
+                    send(U, k, MANY, u_own, u, n - 2)
+
+            each(level_two, MANY)
 
             def level_two_up(k, rows):
                 @pl.when(n + 1 < count)
                 def _():
-                    arrived(XUP, k, x_up)
+                    arrived(XUP, k, MANY, x_up)
 
                 value = wc_next[rows, :] + x_up[rows, :]
                 w_next[rows, :] = value
@@ -381,9 +389,9 @@
 
                 @pl.when(passes)
                 def _():
-                    message(W, k, w, w_next, n - 2).start()
-
-            each(level_two_up)
+                    send(W, k, MANY, w, w_next, n - 2)
+
+            each(level_two_up, MANY)
 
         down(n - 1).start()
         settle(
@@ -399,14 +407,14 @@
         def level_one_up(k, rows):
             @pl.when(jnp.logical_and(chip_even, hears))
             def _():
-                arrived(W, k, w_next)
+                arrived(W, k, FEW, w_next)
 
             value = vc_next[rows, :] + w_next[rows, :]
             e_next[rows, :] = g_next[rows, :] + value
             adj[EVEN, rows, :] = gs[rows, :] + (value + 2.0 * moved(value, EVEN, rows) + r1[rows, :])
-            message(E, k, adj.at[EVEN], e_next, n - 1).start()
-
-        each(level_one_up)
+            send(E, k, FEW, adj.at[EVEN], e_next, n - 1)
+
+        each(level_one_up, FEW)
         value = e_next[...]
         nexts[ODD] = value.astype(BF)
         part = tangent(value, ODD, every)
@@ -415,7 +423,12 @@
         adj[ODD] = value
         nexts[EVEN] = value.astype(BF)
         tang[EVEN] = tangent(value, EVEN, every)
-        settle((XUP, jnp.logical_and(chip_even, n >= 2)), (W, passes), (E, core_one))
+        settle(
+            (XUP, pair_odd),
+            (X_BACK, jnp.logical_and(pair_odd, n + 4 < count)),
+            (W, passes),
+            (E, core_one),
+        )
         down(n).wait_send()
 
 
@@ -445,16 +458,16 @@
         copy.wait()
 
 
-def local(w_in, w_out, checkpoint, guess, terminal, rows_per=64):
+def local(w_in, w_out, checkpoint, guess, terminal):
     count = lax.axis_size("depth")
     pair, width, hidden = w_in.shape
     rows = terminal.shape[0]
-    chunks = rows // rows_per
+    chunks = max(FEW, MANY)
     anywhere = pl.BlockSpec(memory_space=pltpu.HBM)
     inside = pl.BlockSpec(memory_space=pltpu.VMEM)
     plane = pltpu.VMEM((rows, width), F32)
     kept = pl.pallas_call(
-        functools.partial(kernel, count, rows_per),
+        functools.partial(kernel, count),
         out_shape=(
             pltpu.VMEM((pair, rows, hidden), BF),
             pltpu.VMEM((pair, rows, hidden), BF),

time: 63.3 us -> 60.5 us (0.956)
  Pallas kernels: 62.5 us -> 59.8 us
    pallas_call x1, Pallas kernels: 60 us -> 57.2 us  [local(): pl.pallas_call(functools.partial(kernel, count), out_shape=(pltpu.VMEM((p...]
where the time goes in v4:
time: 60.5 us; the launch traced here: 60.4 us
  Pallas kernels  59.8 us (99%)
  between operations  0.64 us (1%)
    pallas_call x1, Pallas kernels, local(): pl.pallas_call(functools.partial(kernel, count), out_shape=(pltpu.VMEM((p...  57.2 us
    pallas_call x1, Pallas kernels, local(): pl.pallas_call(gradients, out_shape=(jax.ShapeDtypeStruct((pair, rows, wi...  2.51 us

profile of v4, /device:TPU:24, one launch (start us, length us, event | category | flops | bytes accessed | tf_op | source)
XLA Modules:
  0.0 60.4 jit_solution(1099257389792951401)
XLA Ops:
  0.6 57.2 %vcycle.1 = (bf16[2,256,1024]{2,1,0:T(8,128)(2,1)S(1)}, bf16[2,256,1024]{2,1,0:T(8,128)(2,1)S(1)}, bf16[2,256,512]{2,1,0:T(8,128)(2,1)S(1)}, bf16[2,256,512]{2,1,0:T(8,128)(2,1)S(1)}, f32[2,256,512]{2,1,0:T(8,128)S(1)}) custom-call(bf16[2,512,1024]{2,1,0:T(8,128)(2,1)} %wi_h.1, bf16[2,1024,512]{2,1,0:T(8,128)(2,1)} %wo_h.1, bf16[1,256,512]{2,1,0:T(8,128)(2,1)} %cp_h.1, ...), custom_call_target="tpu_custom_call" | custom-call | tf_op jit(solution)/shard_map/vcycle/pallas_call | solution.py:469
  57.9 2.5 %gradients.1 = (f32[2,256,512]{2,1,0:T(8,128)}, bf16[2,512,1024]{2,1,0:T(8,128)(2,1)}, bf16[2,1024,512]{2,1,0:T(8,128)(2,1)}) custom-call(bf16[2,256,1024]{2,1,0:T(8,128)(2,1)S(1)} %get-tuple-element.8.tang, bf16[2,256,1024]{2,1,0:T(8,128)(2,1)S(1)} %get-tuple-element.9.act, bf16[2,256,512]{2,1,0:T(8,128)(2,1)S(1)} %get-tuple-element.10.state, ...), custom_call_target="tpu_custom_call" | custom-call | tf_op jit(solution)/shard_map/gradients/pallas_call | solution.py:503

commit v5 on v4

--- a/solution.py
+++ b/solution.py
@@ -15,7 +15,7 @@
 MESSAGES = 14
 FEW, MANY = 4, 8
 PIECES = {kind: MANY if kind in (R2, WC, U, R3, X, XUP, X_BACK, W) else FEW for kind in range(MESSAGES)}
-LAG_TWO, LAG_THREE = 1, 2
+LAG_TWO = 1
 EVEN, ODD, OTHER = 0, 1, 2
 
 
@@ -228,14 +228,13 @@
     def _core_zero():
         each(lambda k, rows: arrived(GUESS_IN, k, FEW, g_next), FEW)
         value = g_next[...]
-        value = value + moved(value, ODD, every)
-        value = value + moved(value, EVEN, every)
-        r1[...] = value - gs[...]
+        r1[...] = value + moved(value, ODD, every)
 
         def level_one(k, rows):
             arrived(R1, k, FEW, r1_next)
             value = r1_next[rows, :]
-            vc[rows, :] = value + 2.0 * moved(value, EVEN, rows) + r1[rows, :]
+            fine_odd = r1[rows, :]
+            vc[rows, :] = value + fine_odd - gs[rows, :] + moved(2.0 * value + fine_odd, EVEN, rows)
 
             @pl.when(n >= 1)
             def _():
@@ -288,28 +287,26 @@
         passes = jnp.logical_and(chip_odd, n + 1 < count)
         hears = n + 3 < count
 
-        def level_one_residual(k, rows):
+        def level_one_change(k, rows):
             @pl.when(n + 1 < count)
             def _():
                 arrived(VC, k, FEW, vc_next)
 
             value = vc_next[rows, :]
-            value = value + 2.0 * moved(value, EVEN, rows)
-            r2[rows, :] = value + 2.0 * moved(value, OTHER, rows)
-
-            @pl.when(passes)
-            def _():
-                send(R2, k, FEW, r2, r2_next, n - 2)
+            return value + 2.0 * moved(value, EVEN, rows)
 
         @pl.when(chip_even)
         def _even_chip():
+            def level_one_residual(k, rows):
+                r2[rows, :] = level_one_change(k, rows)
+
             def level_two(k, rows):
                 @pl.when(hears)
                 def _():
                     arrived(R2, k, MANY, r2_next)
 
-                value = r2_next[rows, :]
-                wc[rows, :] = value + 4.0 * moved(value, OTHER, rows) + r2[rows, :]
+                value, own = r2_next[rows, :], r2[rows, :]
+                wc[rows, :] = value + own + moved(4.0 * value + 2.0 * own, OTHER, rows)
 
                 @pl.when(n >= 2)
                 def _():
@@ -317,33 +314,31 @@
 
             interleaved(level_one_residual, FEW, level_two, MANY, LAG_TWO)
 
-            def level_two_residual(k, rows):
-                @pl.when(hears)
-                def _():
+            @pl.when(pair_even)
+            def _():
+                def level_three(k, rows):
                     arrived(U, k, MANY, u)
-
-                value = u[rows, :]
-                r3[rows, :] = value + 4.0 * moved(value, OTHER, rows)
-
-                @pl.when(pair_odd)
-                def _():
-                    send(R3, k, MANY, r3, r3_next, n - 4)
-
-            @pl.when(pair_even)
-            def _():
-                def level_three(k, rows):
                     arrived(R3, k, MANY, r3_next)
-                    value = r3_next[rows, :]
-                    x[rows, :] = value + 8.0 * moved(value, OTHER, rows) + r3[rows, :]
+                    value, own = r3_next[rows, :], u[rows, :]
+                    x[rows, :] = value + own + moved(8.0 * value + 4.0 * own, OTHER, rows)
 
                     @pl.when(n >= 4)
                     def _():
                         send(X, k, MANY, x, x_next, n - 4)
 
-                interleaved(level_two_residual, MANY, level_three, MANY, LAG_THREE)
+                each(level_three, MANY)
 
             @pl.when(pair_odd)
             def _():
+                def level_two_residual(k, rows):
+                    @pl.when(hears)
+                    def _():
+                        arrived(U, k, MANY, u)
+
+                    value = u[rows, :]
+                    r3[rows, :] = value + 4.0 * moved(value, OTHER, rows)
+                    send(R3, k, MANY, r3, r3_next, n - 4)
+
                 each(level_two_residual, MANY)
 
                 def level_three(k, rows):
@@ -362,6 +357,14 @@
 
         @pl.when(chip_odd)
         def _odd_chip():
+            def level_one_residual(k, rows):
+                value = level_one_change(k, rows)
+                r2[rows, :] = value + 2.0 * moved(value, OTHER, rows)
+
+                @pl.when(passes)
+                def _():
+                    send(R2, k, FEW, r2, r2_next, n - 2)
+
             each(level_one_residual, FEW)
 
             def level_two(k, rows):
@@ -436,6 +439,7 @@
     def transposed_dot(a, b):
         return lax.dot_general(a, b, (((0,), (0,)), ((), ())), preferred_element_type=F32)
 
+    half = go.shape[1] // 2
     stores = [
         pltpu.make_async_copy(source, target, store_sem.at[place])
         for place, (source, target) in enumerate(
@@ -444,16 +448,22 @@
                 (gi.at[0], gi_h.at[0]),
                 (go.at[0], go_h.at[0]),
                 (gi.at[1], gi_h.at[1]),
-                (go.at[1], go_h.at[1]),
+                (go.at[1, pl.ds(0, half)], go_h.at[1, pl.ds(0, half)]),
+                (go.at[1, pl.ds(half, half)], go_h.at[1, pl.ds(half, half)]),
             )
         )
     ]
     stores[0].start()
-    for layer in (0, 1):
-        gi[layer] = transposed_dot(state[layer], tang[layer]).astype(BF)
-        stores[1 + 2 * layer].start()
-        go[layer] = transposed_dot(act[layer], nexts[layer]).astype(BF)
-        stores[2 + 2 * layer].start()
+    gi[0] = transposed_dot(state[0], tang[0]).astype(BF)
+    stores[1].start()
+    go[0] = transposed_dot(act[0], nexts[0]).astype(BF)
+    stores[2].start()
+    gi[1] = transposed_dot(state[1], tang[1]).astype(BF)
+    stores[3].start()
+    for part in (0, 1):
+        some = pl.ds(part * half, half)
+        go[1, some, :] = transposed_dot(act[1, :, some], nexts[1]).astype(BF)
+        stores[4 + part].start()
     for copy in stores:
         copy.wait()
 
@@ -512,7 +522,7 @@
         scratch_shapes=[
             pltpu.VMEM((pair, width, hidden), BF),
             pltpu.VMEM((pair, hidden, width), BF),
-            pltpu.SemaphoreType.DMA((5,)),
+            pltpu.SemaphoreType.DMA((6,)),
         ],
         compiler_params=pltpu.CompilerParams(vmem_limit_bytes=24 << 20),
         name="gradients",

time: 60.5 us -> 58.5 us (0.967)
  Pallas kernels: 59.8 us -> 57.8 us
    pallas_call x1, Pallas kernels: 57.2 us -> 55.3 us  [local(): pl.pallas_call(functools.partial(kernel, count), out_shape=(pltpu.VMEM((p...]
where the time goes in v5:
time: 58.5 us; the launch traced here: 58.4 us
  Pallas kernels  57.8 us (99%)
  between operations  0.64 us (1%)
    pallas_call x1, Pallas kernels, local(): pl.pallas_call(functools.partial(kernel, count), out_shape=(pltpu.VMEM((p...  55.3 us
    pallas_call x1, Pallas kernels, local(): pl.pallas_call(gradients, out_shape=(jax.ShapeDtypeStruct((pair, rows, wi...  2.5 us

profile of v5, /device:TPU:24, one launch (start us, length us, event | category | flops | bytes accessed | tf_op | source)
XLA Modules:
  0.0 58.4 jit_solution(889344491457188175)
XLA Ops:
  0.6 55.3 %vcycle.1 = (bf16[2,256,1024]{2,1,0:T(8,128)(2,1)S(1)}, bf16[2,256,1024]{2,1,0:T(8,128)(2,1)S(1)}, bf16[2,256,512]{2,1,0:T(8,128)(2,1)S(1)}, bf16[2,256,512]{2,1,0:T(8,128)(2,1)S(1)}, f32[2,256,512]{2,1,0:T(8,128)S(1)}) custom-call(bf16[2,512,1024]{2,1,0:T(8,128)(2,1)} %wi_h.1, bf16[2,1024,512]{2,1,0:T(8,128)(2,1)} %wo_h.1, bf16[1,256,512]{2,1,0:T(8,128)(2,1)} %cp_h.1, ...), custom_call_target="tpu_custom_call" | custom-call | tf_op jit(solution)/shard_map/vcycle/pallas_call | solution.py:479
  55.9 2.5 %gradients.1 = (f32[2,256,512]{2,1,0:T(8,128)}, bf16[2,512,1024]{2,1,0:T(8,128)(2,1)}, bf16[2,1024,512]{2,1,0:T(8,128)(2,1)}) custom-call(bf16[2,256,1024]{2,1,0:T(8,128)(2,1)S(1)} %get-tuple-element.8.tang, bf16[2,256,1024]{2,1,0:T(8,128)(2,1)S(1)} %get-tuple-element.9.act, bf16[2,256,512]{2,1,0:T(8,128)(2,1)S(1)} %get-tuple-element.10.state, ...), custom_call_target="tpu_custom_call" | custom-call | tf_op jit(solution)/shard_map/gradients/pallas_call | solution.py:513

commit v6 on v5

--- a/solution.py
+++ b/solution.py
@@ -14,7 +14,7 @@
 GUESS_IN, GUESS, R1, VC, R2, WC, U, R3, X, XUP, X_BACK, W, W_DOWN, E = range(14)
 MESSAGES = 14
 FEW, MANY = 4, 8
-PIECES = {kind: MANY if kind in (R2, WC, U, R3, X, XUP, X_BACK, W) else FEW for kind in range(MESSAGES)}
+PIECES = {kind: MANY if kind in (R1, VC, R2, WC, U, R3, X, XUP, X_BACK, W) else FEW for kind in range(MESSAGES)}
 LAG_TWO = 1
 EVEN, ODD, OTHER = 0, 1, 2
 
@@ -231,16 +231,16 @@
         r1[...] = value + moved(value, ODD, every)
 
         def level_one(k, rows):
-            arrived(R1, k, FEW, r1_next)
+            arrived(R1, k, MANY, r1_next)
             value = r1_next[rows, :]
             fine_odd = r1[rows, :]
             vc[rows, :] = value + fine_odd - gs[rows, :] + moved(2.0 * value + fine_odd, EVEN, rows)
 
             @pl.when(n >= 1)
             def _():
-                send(VC, k, FEW, vc, vc_next, n - 1)
-
-        each(level_one, FEW)
+                send(VC, k, MANY, vc, vc_next, n - 1)
+
+        each(level_one, MANY)
         settle((GUESS, n >= 1), (VC, n >= 1))
         hand_out(n).wait_send()
         hand_in(n).wait_send()

time: 58.5 us -> 58.4 us (level)
  no operation moved by 1% of the time
where the time goes in v6:
time: 58.4 us; the launch traced here: 58.3 us
  Pallas kernels  57.7 us (99%)
  between operations  0.64 us (1%)
    pallas_call x1, Pallas kernels, local(): pl.pallas_call(functools.partial(kernel, count), out_shape=(pltpu.VMEM((p...  55.2 us
    pallas_call x1, Pallas kernels, local(): pl.pallas_call(gradients, out_shape=(jax.ShapeDtypeStruct((pair, rows, wi...  2.5 us

profile of v6, /device:TPU:24, one launch (start us, length us, event | category | flops | bytes accessed | tf_op | source)
XLA Modules:
  0.0 58.3 jit_solution(13685818125009773058)
XLA Ops:
  0.6 55.2 %vcycle.1 = (bf16[2,256,1024]{2,1,0:T(8,128)(2,1)S(1)}, bf16[2,256,1024]{2,1,0:T(8,128)(2,1)S(1)}, bf16[2,256,512]{2,1,0:T(8,128)(2,1)S(1)}, bf16[2,256,512]{2,1,0:T(8,128)(2,1)S(1)}, f32[2,256,512]{2,1,0:T(8,128)S(1)}) custom-call(bf16[2,512,1024]{2,1,0:T(8,128)(2,1)} %wi_h.1, bf16[2,1024,512]{2,1,0:T(8,128)(2,1)} %wo_h.1, bf16[1,256,512]{2,1,0:T(8,128)(2,1)} %cp_h.1, ...), custom_call_target="tpu_custom_call" | custom-call | tf_op jit(solution)/shard_map/vcycle/pallas_call | solution.py:479
  55.8 2.5 %gradients.1 = (f32[2,256,512]{2,1,0:T(8,128)}, bf16[2,512,1024]{2,1,0:T(8,128)(2,1)}, bf16[2,1024,512]{2,1,0:T(8,128)(2,1)}) custom-call(bf16[2,256,1024]{2,1,0:T(8,128)(2,1)S(1)} %get-tuple-element.8.tang, bf16[2,256,1024]{2,1,0:T(8,128)(2,1)S(1)} %get-tuple-element.9.act, bf16[2,256,512]{2,1,0:T(8,128)(2,1)S(1)} %get-tuple-element.10.state, ...), custom_call_target="tpu_custom_call" | custom-call | tf_op jit(solution)/shard_map/gradients/pallas_call | solution.py:513
